TPU v7x, 256 devices: a whole 4x4x8 slice. The times are simulated.
256 devices in a mesh: rows: 64 (over y, z, core), cols: 4 (over x).
Axes of the slice: x: 4, y: 4, z: 8, core: 2. Of those that a mesh axis runs over, the one named last changes fastest.
Arguments:
- residual_block: float32 [524288, 64], P('rows', 'cols'), may hold values from -6 to 6
- basis: bfloat16 [524288, 64], P('rows', 'cols'), may hold values from -0.0078125 to 0.0078125
- fine_tiles: bfloat16 [4096, 4, 128, 128], P('rows')
- fine_index: int32 [4096, 4], P('rows'), may hold values from 0 to 4095, as said below
- mid_tiles: bfloat16 [512, 3, 128, 128], P('rows')
- fine_owner: int32 [524288], P('rows'), may hold values from 0 to 65535, as said below
- mid_owner: int32 [65536], P('rows'), may hold values from 0 to 8191, as said below
- coarse_inverse: float32 [8192, 8192], P('rows'), as said below
Outputs:
- directions: float32 [524288, 64], P('rows', 'cols')
- gram: float32 [64, 64], P(None, 'cols')
Inputs may be any that keep to these rules, and one draw needn't show every extreme that they name: `fine_index`: slot 0 of block row g names g itself; every block named in a block row of partition p (block rows p*64 to p*64 + 63) belongs to partition p - 1, p or p + 1. `fine_owner`: the fine vertices of partition p map to level-one rows p*1024 to p*1024 + 1023; every level-one row receives exactly 8 vertices. `mid_owner`: the level-one rows of partitions 2q and 2q + 1 map to level-two rows 2q*128 to 2q*128 + 2*128 - 1; every level-two row receives exactly 8 level-one rows. coarse_inverse is symmetric.
All inputs are finite; a program needn't handle non-finite values.
Results may differ from a plain program's by a relative error of at most 0.013.
Values may be sent and summed in bfloat16 or wider, within the bound.
A program may use at most 64 MiB of HBM per device.

v0:
```python
import jax
import jax.numpy as jnp
from jax import lax
from jax.sharding import PartitionSpec as P

DAMPING = 0.6666666666666666


def with_halo(array, sides, width):
    for axis, dim in sides:
        peers, length = (lax.axis_size(axis), array.shape[dim])
        up = [(i, (i + 1) % peers) for i in range(peers - 1)]
        down = [(j, i) for i, j in up]
        last = lax.slice_in_dim(array, length - width, length, axis=dim)
        leading = lax.slice_in_dim(array, 0, width, axis=dim)
        before = lax.ppermute(last, axis, up)
        after = lax.ppermute(leading, axis, down)
        array = jnp.concatenate([before, array, after], axis=dim)
    return array


def swapped(value, axis, apart):
    mask = 2**apart
    pairs = [(source, source ^ mask) for source in range(lax.axis_size(axis))]
    return lax.ppermute(value, axis, pairs)


def fine_apply(vector, matrix, window_index):
    extent = matrix.shape[2]
    packed = vector.astype(jnp.bfloat16).reshape(-1, extent, vector.shape[1])
    window = with_halo(packed, (("rows", 0),), packed.shape[0])
    picked = window[window_index]
    product = jnp.einsum("bkij,bkjc->bic", matrix, picked, preferred_element_type=jnp.float32)
    return product.reshape(vector.shape)


def mid_apply(vector, matrix):
    blocks = matrix.shape[0]
    extent = matrix.shape[2]
    packed = vector.astype(jnp.bfloat16).reshape(blocks, extent, vector.shape[1])
    window = with_halo(packed, (("rows", 0),), 1)
    product = jnp.einsum(
        "bij,bjc->bic", matrix[:, 0], window[:-2], preferred_element_type=jnp.float32
    )
    product = product + jnp.einsum(
        "bij,bjc->bic", matrix[:, 1], window[1:-1], preferred_element_type=jnp.float32
    )
    product = product + jnp.einsum(
        "bij,bjc->bic", matrix[:, 2], window[2:], preferred_element_type=jnp.float32
    )
    return product.reshape(vector.shape)


def on_device(
    residual_block, basis, fine_tiles, fine_index, mid_tiles, fine_owner, mid_owner, coarse_inverse
):
    device = lax.axis_index("rows")
    blocks = fine_tiles.shape[0]
    mid_count = mid_tiles.shape[0] * mid_tiles.shape[2]
    coarse_count = coarse_inverse.shape[0]
    col_width = residual_block.shape[1]
    parity = device % 2
    window_index = fine_index - (device - 1) * blocks
    fine_local = fine_owner - device * mid_count
    mid_local = mid_owner - (device - parity) * coarse_count
    fine_inv = 1.0 / jnp.diagonal(fine_tiles[:, 0], axis1=1, axis2=2).astype(jnp.float32).reshape(
        -1, 1
    )
    mid_inv = 1.0 / jnp.diagonal(mid_tiles[:, 1], axis1=1, axis2=2).astype(jnp.float32).reshape(
        -1, 1
    )
    fine_x = DAMPING * fine_inv * residual_block
    fine_x = fine_x + DAMPING * fine_inv * (
        residual_block - fine_apply(fine_x, fine_tiles, window_index)
    )
    fine_res = residual_block - fine_apply(fine_x, fine_tiles, window_index)
    partial_mid = jax.ops.segment_sum(fine_res, fine_local, num_segments=mid_count)
    mid_x = DAMPING * mid_inv * partial_mid
    mid_x = mid_x + DAMPING * mid_inv * (partial_mid - mid_apply(mid_x, mid_tiles))
    mid_res = partial_mid - mid_apply(mid_x, mid_tiles)
    partial_value = jax.ops.segment_sum(mid_res, mid_local, num_segments=2 * coarse_count)
    halves = partial_value.reshape(2, coarse_count, col_width)
    own_half = jnp.where(parity == 0, halves[0], halves[1])
    other_half = jnp.where(parity == 0, halves[1], halves[0])
    coarse_rhs = own_half + swapped(other_half, "rows", 0)
    coarse_fix = jnp.dot(
        coarse_inverse,
        lax.all_gather(coarse_rhs, "rows", axis=0, tiled=True),
        precision=lax.Precision.HIGHEST,
        preferred_element_type=jnp.float32,
    )
    partner_fix = swapped(coarse_fix, "rows", 0)
    pair_values = jnp.where(
        parity == 0,
        jnp.concatenate([coarse_fix, partner_fix], axis=0),
        jnp.concatenate([partner_fix, coarse_fix], axis=0),
    )
    mid_x = mid_x + pair_values[mid_local]
    mid_x = mid_x + DAMPING * mid_inv * (partial_mid - mid_apply(mid_x, mid_tiles))
    fine_x = fine_x + mid_x[fine_local]
    finished = fine_x + DAMPING * fine_inv * (
        residual_block - fine_apply(fine_x, fine_tiles, window_index)
    )
    rounded = finished.astype(jnp.bfloat16)
    partial_gram = lax.dot_general(
        lax.all_gather(basis, "cols", axis=1, tiled=True),
        rounded,
        (((0,), (0,)), ((), ())),
        preferred_element_type=jnp.float32,
    )
    gram = lax.psum(partial_gram, "rows")
    return (finished, gram)


def solution(mesh):
    in_specs = (
        P("rows", "cols"),
        P("rows", "cols"),
        P("rows", None, None, None),
        P("rows", None),
        P("rows", None, None, None),
        P("rows"),
        P("rows"),
        P("rows", None),
    )
    out_specs = (P("rows", "cols"), P(None, "cols"))
    return jax.shard_map(
        on_device, mesh=mesh, in_specs=in_specs, out_specs=out_specs, check_vma=False
    )
```

profile of v0, /device:TPU:1, one launch (start us, length us, event | category | flops | bytes accessed | tf_op | source)
XLA Modules:
  0.0 406.2 jit_solution(2754003155523653004)
XLA Ops:
  7.2 1.5 slice-done
  8.8 3.9 copy.204
  12.7 1.9 gather_fusion
  14.8 4.9 %collective-permute-start = (bf16[64,128,16]{1,2,0:T(8,128)(2,1)S(1)}, bf16[64,128,16]{1,2,0:T(8,128)(2,1)S(1)}, u32[]{:S(2)}, u32[]{:S(2)}) collective-permute-start(bf16[64,128,16]{1,2,0:T(8,128)(2,1)S(1)} %copy_bitcast_fusion.2), channel_id=1, source_target_pairs={{0,4},{4,8},{8,12},{12,16},{16,20},{20,24},{24,28},{28,32},{32,36}... | collective-permute-start | bytes 786440 | tf_op jit(solution)/shard_map/ppermute | solution.py:16
  19.7 1.9 collective-permute-start.1
  21.9 1.0 slice_bitcast_fusion
  22.9 3.1 copy.166
  26.0 1.9 gather_fusion.2
  28.2 0.8 gather_fusion.1
  29.0 5.7 %convolution_bitcast_fusion.2 = f32[64,2,8,128]{3,2,1,0:T(8,128)S(1)} fusion(bf16[64,4,128,16]{2,3,1,0:T(8,128)(2,1)S(1)} %bitcast.177, bf16[64,4,128,128]{3,2,1,0:T(8,128)(2,1)} %param.10), kind=kOutput, calls=%fused_computation.11 | convolution fusion | flops 134217728 | bytes 9961472 | tf_op jit(solution)/shard_map/bkij,bkjc->bic/dot_general | solution.py:33
  34.8 3.6 collective-permute-start.2
  38.5 1.9 collective-permute-start.3
  40.4 1.3 collective-permute-done.2
  41.8 4.4 %collective-permute-done.3 = bf16[64,128,16]{1,2,0:T(8,128)(2,1)S(1)} collective-permute-done((bf16[64,128,16]{1,2,0:T(8,128)(2,1)S(1)}, bf16[64,128,16]{1,2,0:T(8,128)(2,1)S(1)}, u32[]{:S(2)}, u32[]{:S(2)}) %collective-permute-start.3) | collective-permute-done | bytes 262176 | tf_op jit(solution)/shard_map/ppermute | solution.py:17
  46.2 0.8 gather_fusion.3
  47.1 5.7 %convolution_bitcast_fusion.1 = f32[64,2,8,128]{3,2,1,0:T(8,128)S(1)} fusion(bf16[64,4,128,16]{2,3,1,0:T(8,128)(2,1)S(1)} %bitcast.178, bf16[64,4,128,128]{3,2,1,0:T(8,128)(2,1)} %param.10), kind=kOutput, calls=%fused_computation.10 | convolution fusion | flops 134217728 | bytes 9961472 | tf_op jit(solution)/shard_map/bkij,bkjc->bic/dot_general | solution.py:33
  52.8 2.6 copy.172
  55.4 44.4 %scatter_custom_fusion = f32[1024,16]{1,0:T(8,128)S(1)} fusion(s32[8192]{0:T(1024)S(1)} %get-tuple-element.11, f32[8192,16]{1,0:T(8,128)} %copy.172, f32[]{:T(128)} %constant.25.clone.1), kind=kCustom, calls=%fused_computation.51 | custom fusion | flops 131072 | bytes 66048 | tf_op jit(solution)/shard_map/scatter-add | solution.py:77
  100.1 0.2 fusion.65
  100.3 1.9 collective-permute-start.5
  102.3 3.6 collective-permute-start.4
  106.2 0.5 collective-permute-done.4
  107.2 1.9 collective-permute-start.7
  109.1 4.2 %collective-permute-start.6 = (bf16[1,128,16]{1,2,0:T(8,128)(2,1)S(1)}, bf16[1,128,16]{1,2,0:T(8,128)(2,1)S(1)}, u32[]{:S(2)}, u32[]{:S(2)}) collective-permute-start(bf16[1,128,16]{1,2,0:T(8,128)(2,1)S(1)} %get-tuple-element.16), channel_id=1, source_target_pairs={{0,4},{4,8},{8,12},{12,16},{16,20},{20,24},{24,28},{28,32},{32,36}... | collective-permute-start | bytes 12296 | tf_op jit(solution)/shard_map/ppermute | solution.py:16
  113.6 0.5 collective-permute-done.6
  114.5 0.9 bitcast_subtract_fusion.3
  115.4 6.4 %scatter_custom_fusion.1 = f32[256,16]{1,0:T(8,128)S(1)} fusion(s32[1024]{0:T(1024)S(1)} %get-tuple-element.13, f32[1024,16]{1,0:T(8,128)} %bitcast_subtract_fusion.3, f32[]{:T(128)} %constant.25.clone.1), kind=kCustom, calls=%fused_computation.70 | custom fusion | flops 16384 | bytes 16896 | tf_op jit(solution)/shard_map/scatter-add | solution.py:81
  121.8 0.3 collective-permute-start.8
  122.1 1.2 collective-permute-done.8
  123.4 65.2 %all_gather.6 = f32[8192,16]{1,0:T(8,128)S(1)} all-gather(f32[128,16]{1,0:T(8,128)S(1)} %select_add_fusion), channel_id=1, replica_groups=mesh['rows'=64,'cols'=4] {'rows'}, dimensions={0}, use_global_device_ids=true | all-gather | bytes 532480 | tf_op jit(solution)/shard_map/all_gather | solution.py:88
  188.6 6.6 %convolution_bitcast_fusion.4 = f32[128,16]{0,1:T(8,128)S(1)} fusion(f32[8192,16]{1,0:T(8,128)S(1)} %all_gather.6, f32[128,8192]{1,0:T(8,128)S(1)} %copy-done.2), kind=kOutput, calls=%fused_computation.22 | convolution fusion | flops 201326592 | bytes 4726784 | tf_op jit(solution)/shard_map/dot_general | solution.py:86
  195.4 1.0 collective-permute-done.9
  196.5 2.8 gather_fusion.4
  199.5 0.2 fusion.67
  199.7 2.1 collective-permute-start.11
  201.8 3.5 collective-permute-start.10
  205.6 0.5 collective-permute-done.10
  206.5 27.9 %gather_fusion.5 = f32[8192,16]{1,0:T(8,128)} fusion(f32[1024,16]{1,0:T(8,128)S(1)} %copy.193, s32[8192]{0:T(1024)S(1)} %get-tuple-element.10), kind=kCustom, calls=%fused_computation.5 | custom fusion | bytes 1081344 | tf_op jit(solution)/shard_map/gather | solution.py:100
  234.4 2.8 copy.194
  237.4 4.2 %collective-permute-start.12 = (bf16[64,128,16]{1,2,0:T(8,128)(2,1)S(1)}, bf16[64,128,16]{1,2,0:T(8,128)(2,1)S(1)}, u32[]{:S(2)}, u32[]{:S(2)}) collective-permute-start(bf16[64,128,16]{1,2,0:T(8,128)(2,1)S(1)} %copy_bitcast_fusion), channel_id=1, source_target_pairs={{0,4},{4,8},{8,12},{12,16},{16,20},{20,24},{24,28},{28,32},{32,36}... | collective-permute-start | bytes 786440 | tf_op jit(solution)/shard_map/ppermute | solution.py:16
  241.6 1.9 collective-permute-start.13
  243.5 1.3 collective-permute-done.12
  244.8 4.4 %collective-permute-done.13 = bf16[64,128,16]{1,2,0:T(8,128)(2,1)S(1)} collective-permute-done((bf16[64,128,16]{1,2,0:T(8,128)(2,1)S(1)}, bf16[64,128,16]{1,2,0:T(8,128)(2,1)S(1)}, u32[]{:S(2)}, u32[]{:S(2)}) %collective-permute-start.13) | collective-permute-done | bytes 262176 | tf_op jit(solution)/shard_map/ppermute | solution.py:17
  249.3 0.8 gather_fusion.6
  250.2 5.7 %convolution_bitcast_fusion = f32[64,2,8,128]{3,2,1,0:T(8,128)S(1)} fusion(bf16[64,4,128,16]{2,3,1,0:T(8,128)(2,1)S(1)} %bitcast.176, bf16[64,4,128,128]{3,2,1,0:T(8,128)(2,1)} %param.10), kind=kOutput, calls=%fused_computation.9 | convolution fusion | flops 134217728 | bytes 9961472 | tf_op jit(solution)/shard_map/bkij,bkjc->bic/dot_general | solution.py:33
  256.1 13.5 %all-gather.2.cloned.1.call-done = bf16[8192,64]{0,1:T(8,128)(2,1)} async-done(((bf16[8192,16]{0,1:T(8,128)(2,1)}), bf16[8192,64]{0,1:T(8,128)(2,1)}) %all-gather.2.cloned.1.call-update) | async-done | bytes 1048592 | tf_op jit(solution)/shard_map/all_gather | solution.py:106
  269.6 1.6 convolution_bitcast_fusion.3
  271.2 128.1 %psum.7 = f32[64,16]{0,1:T(8,128)} all-reduce(f32[64,16]{0,1:T(8,128)S(1)} %convolution_bitcast_fusion.3), channel_id=1, replica_groups=mesh['rows'=64,'cols'=4] {'rows'}, use_global_device_ids=true, to_apply=%region_2.3 | all-reduce | flops 1024 | bytes 8192 | tf_op jit(solution)/shard_map/psum | solution.py:111
  (67 shorter events, 4.2 us)
Async XLA Ops:
  7.2 1.6 slice-start
  7.2 262.4 %all-gather.2.cloned.1.call-start = ((), (), s32[]{:S(2)}) async-start(), calls=%async_computation | async-start | bytes 1310720 | tf_op jit(solution)/shard_map/all_gather | solution.py:106
  8.8 6.0 %copy-start = (f32[8192,16]{0,1:T(8,128)S(1)}, f32[8192,16]{0,1:T(8,128)}, u32[]{:S(2)}) copy-start(f32[8192,16]{0,1:T(8,128)} %param.8) | copy-start | bytes 1572868
  8.8 12.9 %copy-start.6 = (s32[64,4]{0,1:T(4,128)S(1)}, s32[64,4]{0,1:T(4,128)}, u32[]{:S(2)}) copy-start(s32[64,4]{0,1:T(4,128)} %param.11) | copy-start | bytes 3076
  12.7 15.3 %copy-start.5 = (s32[1024]{0:T(1024)S(1)}, s32[1024]{0:T(1024)}, u32[]{:S(2)}) copy-start(s32[1024]{0:T(1024)} %param.14) | copy-start | bytes 12292
  14.8 13.3 %collective-permute-start = (bf16[64,128,16]{1,2,0:T(8,128)(2,1)S(1)}, bf16[64,128,16]{1,2,0:T(8,128)(2,1)S(1)}, u32[]{:S(2)}, u32[]{:S(2)}) collective-permute-start(bf16[64,128,16]{1,2,0:T(8,128)(2,1)S(1)} %copy_bitcast_fusion.2), channel_id=1, source_target_pairs={{0,4},{4,8},{8,12},{12,16},{16,20},{20,24},{24,28},{28,32},{32,36}... | collective-permute-start | bytes 786440 | tf_op jit(solution)/shard_map/ppermute | solution.py:16
  19.7 8.3 %collective-permute-start.1 = (bf16[64,128,16]{1,2,0:T(8,128)(2,1)S(1)}, bf16[64,128,16]{1,2,0:T(8,128)(2,1)S(1)}, u32[]{:S(2)}, u32[]{:S(2)}) collective-permute-start(bf16[64,128,16]{1,2,0:T(8,128)(2,1)S(1)} %copy_bitcast_fusion.2), channel_id=1, source_target_pairs={{4,0},{8,4},{12,8},{16,12},{20,16},{24,20},{28,24},{32,28},{36,32}... | collective-permute-start | bytes 786440 | tf_op jit(solution)/shard_map/ppermute | solution.py:17
  29.0 11.4 %copy-start.4 = (s32[8192]{0:T(1024)S(1)}, s32[8192]{0:T(1024)}, u32[]{:S(2)}) copy-start(s32[8192]{0:T(1024)} %param.13) | copy-start | bytes 98308
  34.8 6.9 %collective-permute-start.2 = (bf16[64,128,16]{1,2,0:T(8,128)(2,1)S(1)}, bf16[64,128,16]{1,2,0:T(8,128)(2,1)S(1)}, u32[]{:S(2)}, u32[]{:S(2)}) collective-permute-start(bf16[64,128,16]{1,2,0:T(8,128)(2,1)S(1)} %copy_bitcast_fusion.1), channel_id=1, source_target_pairs={{0,4},{4,8},{8,12},{12,16},{16,20},{20,24},{24,28},{28,32},{32,36}... | collective-permute-start | bytes 786440 | tf_op jit(solution)/shard_map/ppermute | solution.py:16
  38.5 7.7 %collective-permute-start.3 = (bf16[64,128,16]{1,2,0:T(8,128)(2,1)S(1)}, bf16[64,128,16]{1,2,0:T(8,128)(2,1)S(1)}, u32[]{:S(2)}, u32[]{:S(2)}) collective-permute-start(bf16[64,128,16]{1,2,0:T(8,128)(2,1)S(1)} %copy_bitcast_fusion.1), channel_id=1, source_target_pairs={{4,0},{8,4},{12,8},{16,12},{20,16},{24,20},{28,24},{32,28},{36,32}... | collective-permute-start | bytes 786440 | tf_op jit(solution)/shard_map/ppermute | solution.py:17
  52.8 47.3 %copy-start.1 = (bf16[8,3,128,128]{3,2,1,0:T(8,128)(2,1)S(1)}, bf16[8,3,128,128]{3,2,1,0:T(8,128)(2,1)}, u32[]{:S(2)}) copy-start(bf16[8,3,128,128]{3,2,1,0:T(8,128)(2,1)} %param.12) | copy-start | bytes 2359300
  100.3 5.6 %collective-permute-start.5 = (bf16[1,128,16]{1,2,0:T(8,128)(2,1)S(1)}, bf16[1,128,16]{1,2,0:T(8,128)(2,1)S(1)}, u32[]{:S(2)}, u32[]{:S(2)}) collective-permute-start(bf16[1,128,16]{1,2,0:T(8,128)(2,1)S(1)} %get-tuple-element.19), channel_id=1, source_target_pairs={{4,0},{8,4},{12,8},{16,12},{20,16},{24,20},{28,24},{32,28},{36,32}... | collective-permute-start | bytes 12296 | tf_op jit(solution)/shard_map/ppermute | solution.py:17
  102.3 4.4 %collective-permute-start.4 = (bf16[1,128,16]{1,2,0:T(8,128)(2,1)S(1)}, bf16[1,128,16]{1,2,0:T(8,128)(2,1)S(1)}, u32[]{:S(2)}, u32[]{:S(2)}) collective-permute-start(bf16[1,128,16]{1,2,0:T(8,128)(2,1)S(1)} %get-tuple-element.18), channel_id=1, source_target_pairs={{0,4},{4,8},{8,12},{12,16},{16,20},{20,24},{24,28},{28,32},{32,36}... | collective-permute-start | bytes 12296 | tf_op jit(solution)/shard_map/ppermute | solution.py:16
  107.2 6.1 %collective-permute-start.7 = (bf16[1,128,16]{1,2,0:T(8,128)(2,1)S(1)}, bf16[1,128,16]{1,2,0:T(8,128)(2,1)S(1)}, u32[]{:S(2)}, u32[]{:S(2)}) collective-permute-start(bf16[1,128,16]{1,2,0:T(8,128)(2,1)S(1)} %get-tuple-element.17), channel_id=1, source_target_pairs={{4,0},{8,4},{12,8},{16,12},{20,16},{24,20},{28,24},{32,28},{36,32}... | collective-permute-start | bytes 12296 | tf_op jit(solution)/shard_map/ppermute | solution.py:17
  109.1 4.9 %collective-permute-start.6 = (bf16[1,128,16]{1,2,0:T(8,128)(2,1)S(1)}, bf16[1,128,16]{1,2,0:T(8,128)(2,1)S(1)}, u32[]{:S(2)}, u32[]{:S(2)}) collective-permute-start(bf16[1,128,16]{1,2,0:T(8,128)(2,1)S(1)} %get-tuple-element.16), channel_id=1, source_target_pairs={{0,4},{4,8},{8,12},{12,16},{16,20},{20,24},{24,28},{28,32},{32,36}... | collective-permute-start | bytes 12296 | tf_op jit(solution)/shard_map/ppermute | solution.py:16
  121.8 66.8 %copy-start.2 = (f32[128,8192]{1,0:T(8,128)S(1)}, f32[128,8192]{1,0:T(8,128)}, u32[]{:S(2)}) copy-start(f32[128,8192]{1,0:T(8,128)} %param.15) | copy-start | bytes 12582916
  121.8 1.5 collective-permute-start.8
  195.2 1.2 collective-permute-start.9
  199.7 5.6 %collective-permute-start.11 = (bf16[1,128,16]{1,2,0:T(8,128)(2,1)S(1)}, bf16[1,128,16]{1,2,0:T(8,128)(2,1)S(1)}, u32[]{:S(2)}, u32[]{:S(2)}) collective-permute-start(bf16[1,128,16]{1,2,0:T(8,128)(2,1)S(1)} %get-tuple-element.15), channel_id=1, source_target_pairs={{4,0},{8,4},{12,8},{16,12},{20,16},{24,20},{28,24},{32,28},{36,32}... | collective-permute-start | bytes 12296 | tf_op jit(solution)/shard_map/ppermute | solution.py:17
  201.8 4.2 %collective-permute-start.10 = (bf16[1,128,16]{1,2,0:T(8,128)(2,1)S(1)}, bf16[1,128,16]{1,2,0:T(8,128)(2,1)S(1)}, u32[]{:S(2)}, u32[]{:S(2)}) collective-permute-start(bf16[1,128,16]{1,2,0:T(8,128)(2,1)S(1)} %get-tuple-element.14), channel_id=1, source_target_pairs={{0,4},{4,8},{8,12},{12,16},{16,20},{20,24},{24,28},{28,32},{32,36}... | collective-permute-start | bytes 12296 | tf_op jit(solution)/shard_map/ppermute | solution.py:16
  237.4 7.5 %collective-permute-start.12 = (bf16[64,128,16]{1,2,0:T(8,128)(2,1)S(1)}, bf16[64,128,16]{1,2,0:T(8,128)(2,1)S(1)}, u32[]{:S(2)}, u32[]{:S(2)}) collective-permute-start(bf16[64,128,16]{1,2,0:T(8,128)(2,1)S(1)} %copy_bitcast_fusion), channel_id=1, source_target_pairs={{0,4},{4,8},{8,12},{12,16},{16,20},{20,24},{24,28},{28,32},{32,36}... | collective-permute-start | bytes 786440 | tf_op jit(solution)/shard_map/ppermute | solution.py:16
  241.6 7.7 %collective-permute-start.13 = (bf16[64,128,16]{1,2,0:T(8,128)(2,1)S(1)}, bf16[64,128,16]{1,2,0:T(8,128)(2,1)S(1)}, u32[]{:S(2)}, u32[]{:S(2)}) collective-permute-start(bf16[64,128,16]{1,2,0:T(8,128)(2,1)S(1)} %copy_bitcast_fusion), channel_id=1, source_target_pairs={{4,0},{8,4},{12,8},{16,12},{20,16},{24,20},{28,24},{32,28},{36,32}... | collective-permute-start | bytes 786440 | tf_op jit(solution)/shard_map/ppermute | solution.py:17
  256.1 143.3 %copy-start.3 = (f32[8192,16]{0,1:T(8,128)}, f32[8192,16]{0,1:T(8,128)S(1)}, u32[]{:S(2)}) copy-start(f32[8192,16]{0,1:T(8,128)S(1)} %fusion.7) | copy-start | bytes 1572868
Sparse Core Ops, SparseCore 0:
  243.6 25.9 all-gather.1
where the time goes:
time: 409 us; the launch traced here: 406 us
  blocking collectives  193 us (47%)
  local copies, waits for them, and re-layouts  53.3 us (13%)
  other arithmetic  52.8 us (13%)
  starting transfers between devices  36.3 us (9%)
  waiting for transfers between devices  28.7 us (7%)
  matrix products  27.3 us (7%)
  between operations  14.5 us (4%)
    psum x1, blocking collectives, on_device(): gram = lax.psum(partial_gram, 'rows')  128 us
    all_gather x1, blocking collectives, on_device(): lax.all_gather(coarse_rhs, 'rows', axis=0, tiled=True)  65.2 us
    scatter-add x1, other arithmetic, on_device(): jax.ops.segment_sum(fine_res, fine_local, num_segments=mid_count)  44.4 us
    gather x2, local copies, waits for them, and re-layouts, on_device(): fine_x = fine_x + mid_x[fine_local]  30.7 us
    ppermute x6, starting transfers between devices, with_halo(): before = lax.ppermute(last, axis, up)  24.1 us
    dot_general x3, matrix products, fine_apply(): jnp.einsum('bkij,bkjc->bic', matrix, picked, preferred_element_type=jnp.f...  17 us
    all_gather x1, waiting for transfers between devices, on_device(): lax.all_gather(basis, 'cols', axis=1, tiled=True)  13.5 us
    ppermute x6, starting transfers between devices, with_halo(): after = lax.ppermute(leading, axis, down)  11.7 us
  transfers between devices with their start and end apart: 15, of which 10 were waited for; matrix products, arithmetic and copies ran while one was open for 3% of the time, Pallas kernels for 0%

commit v1 on v0

v1 whole, which is shorter than its diff:
```python
import functools

import jax
import jax.numpy as jnp
from jax import lax
from jax.experimental import pallas as pl
from jax.experimental.pallas import tpu as pltpu
from jax.sharding import PartitionSpec as P

W = 0.6666666666666666
NT = (((1,), (1,)), ((), ()))
NN = (((1,), (0,)), ((), ()))
F32 = jnp.float32
BF = jnp.bfloat16
L = 128
QUARTERS = 4


def dot(a, b, dims):
    return lax.dot_general(a, b, dims, preferred_element_type=F32)


def split(x):
    high = x.astype(BF)
    return high, (x - high.astype(F32)).astype(BF)


def kernel(
    ny, nz, nx,
    res_hbm, basis_hbm, tiles_hbm, idx_ref, mid_hbm, own_hbm, mown_hbm, coarse_hbm,
    dir_ref, gram_ref,
    res_v, tiles_v, mid_v, own_v, mown_v, coarse_v, cb_v, basis_v, scale_v, x_v, fr_v,
    win1, win2, win3, oht, oh2t, ms_v, mwin1, mwin2, mwin3, pair1, pair2, ag, cw, dirb,
    ga, gz, gy,
    lsem, hs, hr, msend, mrecv, psend, precv, ags, agr, bs, br, gs, gr,
):
    nb = tiles_v.shape[0]
    nm = mid_v.shape[0]
    nch = ny * nz
    rows = 2 * nch
    cdev = coarse_v.shape[0]
    cols = res_v.shape[0]
    r = lax.axis_index("rows")
    x = lax.axis_index("cols")
    core = lax.rem(r, 2)
    chip = r // 2
    zc = lax.rem(chip, nz)
    yc = chip // nz
    right = lax.rem(r + 1, rows)
    left = lax.rem(r + rows - 1, rows)
    partner = 2 * chip + 1 - core
    outer = lax.rem(r + 2 * core - 1 + rows, rows)

    def remote(src, dst, ssem, rsem, where):
        return pltpu.make_async_remote_copy(
            src_ref=src, dst_ref=dst, send_sem=ssem, recv_sem=rsem,
            device_id=where, device_id_type=pl.DeviceIdType.MESH,
        )

    def local(src, dst, k):
        return pltpu.make_async_copy(src, dst, lsem.at[k])

    def lanes(g, n=1):
        return pl.ds(pl.multiple_of(g * L, L), n * L)

    diag_in = local(tiles_hbm.at[:, 0], tiles_v.at[:, 0], 0)
    res_in = local(res_hbm, res_v, 1)
    off_in = local(tiles_hbm.at[:, 1:4], tiles_v.at[:, 1:4], 2)
    own_in = local(own_hbm, own_v, 3)
    mown_in = local(mown_hbm, mown_v, 4)
    mid_in = local(mid_hbm, mid_v, 5)
    coarse_in = local(coarse_hbm, coarse_v, 6)
    basis_in = local(basis_hbm, basis_v.at[x], 7)
    for copy in (diag_in, res_in, own_in, mown_in, off_in, mid_in, coarse_in, basis_in):
        copy.start()

    barrier = pltpu.get_barrier_semaphore()

    def greet(where):
        pl.semaphore_signal(
            barrier, inc=1, device_id=where, device_id_type=pl.DeviceIdType.MESH
        )

    greet({"rows": partner})
    greet({"rows": outer})

    @pl.loop(1, nch)
    def _(d):
        greet({"rows": 2 * lax.rem(chip + d, nch) + core})

    @pl.loop(1, nx)
    def _(d):
        greet({"cols": lax.rem(x + d, nx)})

    eye = lax.broadcasted_iota(jnp.int32, (L, L), 0) == lax.broadcasted_iota(
        jnp.int32, (L, L), 1
    )

    def weight(tile):
        d = jnp.sum(jnp.where(eye, tile.astype(F32), 0.0), axis=0, keepdims=True)
        return jnp.broadcast_to(W * (1.0 / d), (cols, L))

    diag_in.wait()
    res_in.wait()

    def first(g, carry):
        s = weight(tiles_v[g, 0])
        scale_v[g] = s
        win1[nb + g] = (s * res_v[:, lanes(g)]).astype(BF)
        return carry

    lax.fori_loop(0, nb, first, 0, unroll=4)

    def halo(win, k, lo, n):
        return (
            remote(win.at[pl.ds(nb + lo, n)], win.at[pl.ds(lo, n)], hs.at[k, 0], hr.at[k, 0], {"rows": right}),
            remote(win.at[pl.ds(nb + lo, n)], win.at[pl.ds(2 * nb + lo, n)], hs.at[k, 1], hr.at[k, 1], {"rows": left}),
        )

    def halo_start(win, k, lo, n):
        for copy in halo(win, k, lo, n):
            copy.start()

    def halo_wait(win, k):
        for copy in halo(win, k, 0, nb):
            copy.wait_recv()

    pl.semaphore_wait(barrier, nch - 1 + 2 + nx - 1)
    halo_start(win1, 0, 0, nb)

    basis_in.wait()

    def basis_copy(d):
        return remote(
            basis_v.at[x], basis_v.at[x], bs, br, {"cols": lax.rem(x + d, nx)}
        )

    @pl.loop(1, nx)
    def _(d):
        basis_copy(d).start()

    own_in.wait()
    mown_in.wait()
    mid_in.wait()
    low_iota = lax.broadcasted_iota(jnp.int32, (L, L), 0)
    fine_base = r * (nm * L)

    def owner_row(g):
        return own_v[pl.ds(g, 1), :] - fine_base

    def hot(g, carry):
        low = jnp.bitwise_and(owner_row(g), L - 1)
        oht[:, lanes(g)] = jnp.where(low_iota == low, 1.0, 0.0).astype(BF)
        return carry

    lax.fori_loop(0, nb, hot, 0, unroll=4)
    wide_iota = lax.broadcasted_iota(jnp.int32, (2 * cdev, L), 0)
    mid_base = (r - core) * cdev
    for g in range(nm):
        oh2t[:, g * L : (g + 1) * L] = jnp.where(
            wide_iota == mown_v[g : g + 1, :] - mid_base, 1.0, 0.0
        ).astype(BF)
        ms_v[g] = weight(mid_v[g, 1])

    off_in.wait()
    halo_wait(win1, 0)
    base = (r - 1) * nb

    def product(win, g):
        picked = [win[nb + g]] + [
            win[jnp.clip(idx_ref[s, g] - base, 0, 3 * nb - 1)] for s in (1, 2, 3)
        ]
        tile = [tiles_v[g, s] for s in range(4)]
        return dot(jnp.concatenate(picked, axis=1), jnp.concatenate(tile, axis=1), NT)

    def fine_b(g, carry):
        s = scale_v[g]
        rhs = res_v[:, lanes(g)]
        v = s * rhs + s * (rhs - product(win1, g))
        x_v[g] = v
        win2[nb + g] = v.astype(BF)
        return carry

    step = nb // QUARTERS
    for q in range(QUARTERS):
        lax.fori_loop(q * step, (q + 1) * step, fine_b, 0, unroll=min(8, step))
        halo_start(win2, 1, q * step, step)

    coarse_in.wait()

    def convert(c, carry):
        for k in range(2):
            at = pl.multiple_of((2 * c + k) * cdev, cdev)
            cb_v[k, c] = coarse_v[:, pl.ds(at, cdev)].astype(BF)
        return carry

    lax.fori_loop(0, nch, convert, 0, unroll=2)
    halo_wait(win2, 1)

    def residual(g, carry):
        fr_v[g] = res_v[:, lanes(g)] - product(win2, g)
        return carry

    lax.fori_loop(0, nb, residual, 0, unroll=8)

    def restrict(c, acc):
        parts = []
        for k in range(4):
            g = 4 * c + k
            high = jnp.broadcast_to(lax.shift_right_logical(owner_row(g), 7), (cols, L))
            v = fr_v[g]
            parts.append(
                jnp.concatenate(
                    [jnp.where(high == h, v, 0.0).astype(BF) for h in range(nm)], axis=0
                )
            )
        return acc + dot(jnp.concatenate(parts, axis=1), oht[:, lanes(4 * c, 4)], NT)

    mid_rhs = lax.fori_loop(
        0, nb // 4, restrict, jnp.zeros((nm * cols, L), F32), unroll=2
    ).reshape(nm, cols, L)

    ms = ms_v[...]

    def mid_halo(mwin, k):
        return (
            remote(mwin.at[nm], mwin.at[0], msend.at[k, 0], mrecv.at[k, 0], {"rows": right}),
            remote(mwin.at[1], mwin.at[nm + 1], msend.at[k, 1], mrecv.at[k, 1], {"rows": left}),
        )

    def mid_product(v, mwin, k):
        mwin[1 : nm + 1] = v.astype(BF)
        for copy in mid_halo(mwin, k):
            copy.start()
        for copy in mid_halo(mwin, k):
            copy.wait_recv()
        zero = jnp.zeros((cols, L), BF)
        mwin[0] = jnp.where(r > 0, mwin[0], zero)
        mwin[nm + 1] = jnp.where(r < rows - 1, mwin[nm + 1], zero)
        out = []
        for g in range(nm):
            v3 = jnp.concatenate([mwin[g + k] for k in range(3)], axis=1)
            t3 = jnp.concatenate([mid_v[g, k] for k in range(3)], axis=1)
            out.append(dot(v3, t3, NT))
        return jnp.stack(out)

    mid_x = ms * mid_rhs
    mid_x = mid_x + ms * (mid_rhs - mid_product(mid_x, mwin1, 0))
    mid_res = mid_rhs - mid_product(mid_x, mwin2, 1)

    def flat(v):
        return jnp.concatenate([v[g] for g in range(nm)], axis=1)

    both = dot(jnp.concatenate(split(flat(mid_res)), axis=0), oh2t[...], NT)
    partial = both[:cols] + both[cols:]
    even, odd = partial[:, :cdev], partial[:, cdev:]
    pair1[0] = jnp.where(core == 0, odd, even)
    swap1 = remote(pair1.at[0], pair1.at[1], psend.at[0], precv.at[0], {"rows": partner})
    swap1.start()
    swap1.wait_recv()
    coarse_rhs = jnp.where(core == 0, even, odd) + pair1[1]

    ag[core, chip] = coarse_rhs.astype(BF)

    def ag_copy(d):
        return remote(
            ag.at[core, chip], ag.at[core, chip], ags.at[0], agr.at[0],
            {"rows": 2 * lax.rem(chip + d, nch) + core},
        )

    @pl.loop(1, nch)
    def _(d):
        ag_copy(d).start()

    def ag_rest(slot):
        return remote(
            ag.at[slot, pl.ds(0, nch - 1)], ag.at[slot, pl.ds(0, nch - 1)],
            ags.at[0], agr.at[0], {"rows": partner},
        )

    ag_rest(core).wait_recv()
    half = remote(ag.at[core], ag.at[core], ags.at[1], agr.at[1], {"rows": partner})
    half.start()

    def coarse_half(k, acc):
        def chunk(c, acc):
            v = jnp.concatenate([ag[k, 4 * c + i] for i in range(4)], axis=1)
            t = jnp.concatenate([cb_v[k, 4 * c + i] for i in range(4)], axis=1)
            return acc + dot(v, t, NT)

        return lax.fori_loop(0, nch // 4, chunk, acc, unroll=min(4, nch // 4))

    fix = coarse_half(core, jnp.zeros((cols, cdev), F32))
    half.wait_recv()
    fix = coarse_half(1 - core, fix)

    pair2[0] = fix
    swap2 = remote(pair2.at[0], pair2.at[1], psend.at[1], precv.at[1], {"rows": partner})
    swap2.start()
    swap2.wait_recv()
    other = pair2[1]
    values = jnp.concatenate(
        [jnp.where(core == 0, fix, other), jnp.where(core == 0, other, fix)], axis=1
    )
    both = dot(jnp.concatenate(split(values), axis=0), oh2t[...], NN)
    lift = both[:cols] + both[cols:]
    mid_x = mid_x + jnp.stack([lift[:, g * L : (g + 1) * L] for g in range(nm)])
    mid_x = mid_x + ms * (mid_rhs - mid_product(mid_x, mwin3, 2))

    md = mid_x.reshape(nm * cols, L)
    cw[...] = jnp.concatenate(split(md), axis=1)

    def prolong(c, carry):
        hot4 = oht[:, lanes(4 * c, 4)]
        up = dot(cw[...], jnp.concatenate([hot4, hot4], axis=0), NN)
        for k in range(4):
            g = 4 * c + k
            high = jnp.broadcast_to(lax.shift_right_logical(owner_row(g), 7), (cols, L))
            v = x_v[g]
            for h in range(nm):
                v = v + jnp.where(
                    high == h, up[h * cols : (h + 1) * cols, k * L : (k + 1) * L], 0.0
                )
            x_v[g] = v
            win3[nb + g] = v.astype(BF)
        return carry

    for q in range(QUARTERS):
        lax.fori_loop(q * step // 4, (q + 1) * step // 4, prolong, 0, unroll=min(2, step // 4))
        halo_start(win3, 2, q * step, step)
    halo_wait(win3, 2)

    def finish(g, carry):
        v = x_v[g] + scale_v[g] * (res_v[:, lanes(g)] - product(win3, g))
        dir_ref[:, lanes(g)] = v
        dirb[:, lanes(g)] = v.astype(BF)
        return carry

    lax.fori_loop(0, nb, finish, 0, unroll=8)

    def basis_rest():
        return remote(
            basis_v.at[pl.ds(0, nx - 1)], basis_v.at[pl.ds(0, nx - 1)], bs, br,
            {"rows": partner},
        )

    basis_rest().wait_recv()

    def gram(c, acc):
        t = basis_v[:, :, lanes(4 * c, 4)].reshape(nx * cols, 4 * L)
        return acc + dot(dirb[:, lanes(4 * c, 4)], t, NT)

    total = lax.fori_loop(
        0, nb // 4, gram, jnp.zeros((cols, nx * cols), F32), unroll=min(4, nb // 4)
    )
    rows8 = cols // 2
    ga[core] = jnp.concatenate([total[:rows8], total[rows8:]], axis=1)
    swap3 = remote(ga.at[core], ga.at[core], gs.at[0], gr.at[0], {"rows": partner})
    swap3.start()
    swap3.wait_recv()
    gz[zc] = ga[0] + ga[1]

    def z_copy(d):
        to = 2 * (yc * nz + lax.rem(zc + d, nz)) + core
        return remote(gz.at[zc], gz.at[zc], gs.at[1], gr.at[1], {"rows": to})

    def y_copy(d):
        to = 2 * (lax.rem(yc + d, ny) * nz + zc) + core
        return remote(gy.at[yc], gy.at[yc], gs.at[2], gr.at[2], {"rows": to})

    def rest(buf, k, n):
        return remote(
            buf.at[pl.ds(0, n - 1)], buf.at[pl.ds(0, n - 1)], gs.at[k], gr.at[k],
            {"rows": partner},
        )

    @pl.loop(1, nz)
    def _(d):
        z_copy(d).start()

    rest(gz, 1, nz).wait_recv()
    acc = gz[0]
    for k in range(1, nz):
        acc = acc + gz[k]
    gy[yc] = acc

    @pl.loop(1, ny)
    def _(d):
        y_copy(d).start()

    rest(gy, 2, ny).wait_recv()
    acc = gy[0]
    for k in range(1, ny):
        acc = acc + gy[k]
    wide = nx * cols
    gram_ref[...] = jnp.concatenate([acc[:, :wide], acc[:, wide:]], axis=0)

    for k, win in enumerate((win1, win2, win3)):
        for copy in halo(win, k, 0, nb):
            copy.wait_send()
    for k, mwin in enumerate((mwin1, mwin2, mwin3)):
        for copy in mid_halo(mwin, k):
            copy.wait_send()
    for copy in (swap1, swap2, swap3, half, ag_rest(core), basis_rest(), rest(gz, 1, nz), rest(gy, 2, ny)):
        copy.wait_send()


def on_device(ny, nz, nx, residual, basis, fine_tiles, fine_index, mid_tiles, fine_owner, mid_owner, coarse):
    nb = fine_tiles.shape[0]
    nm = mid_tiles.shape[0]
    cols = residual.shape[1]
    cdev = coarse.shape[0]
    n = nb * L
    nch = ny * nz
    vm, dma = pltpu.VMEM, pltpu.SemaphoreType.DMA
    scratch = [
        vm((cols, n), F32), vm((nb, 4, L, L), BF), vm((nm, 3, L, L), BF),
        vm((nb, L), jnp.int32), vm((nm, L), jnp.int32),
        vm(coarse.shape, F32), vm((2, nch, cdev, cdev), BF), vm((nx, cols, n), BF),
        vm((nb, cols, L), F32), vm((nb, cols, L), F32), vm((nb, cols, L), F32),
        vm((3 * nb, cols, L), BF), vm((3 * nb, cols, L), BF), vm((3 * nb, cols, L), BF),
        vm((L, n), BF), vm((2 * cdev, nm * L), BF), vm((nm, cols, L), F32),
        vm((nm + 2, cols, L), BF), vm((nm + 2, cols, L), BF), vm((nm + 2, cols, L), BF),
        vm((2, cols, cdev), F32), vm((2, cols, cdev), F32), vm((2, nch, cols, cdev), BF),
        vm((nm * cols, 2 * L), BF), vm((cols, n), BF),
        vm((2, cols // 2, 2 * nx * cols), F32), vm((nz, cols // 2, 2 * nx * cols), F32),
        vm((ny, cols // 2, 2 * nx * cols), F32),
        dma((8,)), dma((3, 2)), dma((3, 2)), dma((3, 2)), dma((3, 2)), dma((2,)), dma((2,)),
        dma((2,)), dma((2,)), dma, dma, dma((3,)), dma((3,)),
    ]
    hbm = pl.BlockSpec(memory_space=pl.ANY)
    vmem = pl.BlockSpec(memory_space=pltpu.VMEM)
    directions, gram = pl.pallas_call(
        functools.partial(kernel, ny, nz, nx),
        out_shape=(
            jax.ShapeDtypeStruct((cols, n), F32),
            jax.ShapeDtypeStruct((cols, nx * cols), F32),
        ),
        in_specs=[hbm, hbm, hbm, pl.BlockSpec(memory_space=pltpu.SMEM), hbm, hbm, hbm, hbm],
        out_specs=(vmem, vmem),
        scratch_shapes=scratch,
        name="vcycle",
        compiler_params=pltpu.CompilerParams(
            collective_id=0, has_side_effects=True, vmem_limit_bytes=56 * 2**20
        ),
    )(
        residual.T, basis.T, fine_tiles, fine_index.T, mid_tiles,
        fine_owner.reshape(nb, L), mid_owner.reshape(nm, L), coarse,
    )
    return directions.T, gram.T


def solution(mesh, ny=4, nz=8):
    in_specs = (
        P("rows", "cols"),
        P("rows", "cols"),
        P("rows", None, None, None),
        P("rows", None),
        P("rows", None, None, None),
        P("rows"),
        P("rows"),
        P("rows", None),
    )
    out_specs = (P("rows", "cols"), P(None, "cols"))
    return jax.shard_map(
        functools.partial(on_device, ny, nz, mesh.shape["cols"]),
        mesh=mesh, in_specs=in_specs, out_specs=out_specs, check_vma=False,
    )
```

time: 409 us -> 74.8 us (0.18)
  blocking collectives: 193 us -> 0 us
  Pallas kernels: 0 us -> 70.8 us
  other arithmetic: 52.8 us -> 0 us
  local copies, waits for them, and re-layouts: 53.3 us -> 3.16 us
  starting transfers between devices: 36.3 us -> 0 us
  waiting for transfers between devices: 28.7 us -> 0 us
  matrix products: 27.3 us -> 0 us
  between operations: 14.5 us -> 0.64 us
    psum x1 -> x0, blocking collectives: 128 us -> none  [on_device(): gram = lax.psum(partial_gram, 'rows')]
    pallas_call x0 -> x1, Pallas kernels: none -> 70.8 us  [on_device(): pl.pallas_call(functools.partial(kernel, ny, nz, nx), out_shape=(jax.Shap...]
    all_gather x1 -> x0, blocking collectives: 65.2 us -> none  [on_device(): lax.all_gather(coarse_rhs, 'rows', axis=0, tiled=True)]
    scatter-add x2 -> x0, other arithmetic: 50.9 us -> none  [the longest x1 44.4 us: on_device(): jax.ops.segment_sum(fine_res, fine_local, num_segments=mid_count)]
    gather x10 -> x0, local copies, waits for them, and re-layouts: 40.1 us -> none  [the longest x2 30.7 us: on_device(): fine_x = fine_x + mid_x[fine_local]]
    ppermute x14 -> x0, starting transfers between devices: 36.2 us -> none  [the longest x6 24.1 us: with_halo(): before = lax.ppermute(last, axis, up)]
    dot_general x14 -> x0, matrix products: 27.3 us -> none  [the longest x3 17 us: fine_apply(): jnp.einsum('bkij,bkjc->bic', matrix, picked, preferred_element_type=jnp.f...]
    ppermute x14 -> x0, waiting for transfers between devices: 15.2 us -> none  [the longest x6 8.8 us: with_halo(): after = lax.ppermute(leading, axis, down)]
  transfers between devices with their start and end apart: 15 -> 0, of which waited for: 10 -> 0; matrix products, arithmetic and copies ran while one was open for 3% -> 0% of each run, Pallas kernels for 0% -> 0%
where the time goes in v1:
time: 74.8 us; the launch traced here: 74.6 us
  Pallas kernels  70.8 us (95%)
  local copies, waits for them, and re-layouts  3.16 us (4%)
    pallas_call x1, Pallas kernels, on_device(): pl.pallas_call(functools.partial(kernel, ny, nz, nx), out_shape=(jax.Shap...  70.8 us
    unnamed x2, local copies, waits for them, and re-layouts  3.16 us

profile of v1, /device:TPU:1, one launch (start us, length us, event | category | flops | bytes accessed | tf_op | source)
XLA Modules:
  0.0 74.6 jit_solution(12034827518977875374)
XLA Ops:
  0.6 70.8 %vcycle.1 = (f32[16,8192]{1,0:T(8,128)}, f32[16,64]{1,0:T(8,128)}) custom-call(f32[16,8192]{1,0:T(8,128)} %bitcast.7, bf16[16,8192]{1,0:T(8,128)(2,1)} %bitcast.9, bf16[64,4,128,128]{3,2,1,0:T(8,128)(2,1)} %tiles_hbm.1, s32[4,64]{1,0:T(4,128)} %bitcast.13, bf16[8,3,128,128]{3,2,1,0:T(8,128)(2,1)} %mid_hbm.1, s32[64,128]{1,0:T(8,128)} %bitcast.10, ...), custom_call_target="tpu_custom_call" | custom-call | tf_op jit(solution)/shard_map/vcycle/pallas_call | solution.py:433
  71.4 1.9 %copy.12 = f32[8192,16]{0,1:T(8,128)} copy(f32[8192,16]{0,1:T(8,128)} %bitcast.8) | data formatting | bytes 1048576
  73.3 1.3 %copy.13 = f32[64,16]{0,1:T(8,128)} copy(f32[64,16]{0,1:T(8,128)} %bitcast.11) | data formatting | bytes 8192

commit v2 on v1

v2 whole, which is shorter than its diff:
```python
import functools

import jax
import jax.numpy as jnp
from jax import lax
from jax.experimental import pallas as pl
from jax.experimental.pallas import tpu as pltpu
from jax.sharding import PartitionSpec as P

W = 0.6666666666666666
NT = (((1,), (1,)), ((), ()))
NN = (((1,), (0,)), ((), ()))
F32 = jnp.float32
BF = jnp.bfloat16
L = 128
QUARTERS = 4


def dot(a, b, dims):
    return lax.dot_general(a, b, dims, preferred_element_type=F32)


def split(x):
    high = x.astype(BF)
    return high, (x - high.astype(F32)).astype(BF)


def kernel(
    ny, nz, nx,
    res_hbm, basis_hbm, tiles_hbm, idx_ref, mid_hbm, own_hbm, mown_hbm, coarse_hbm,
    dir_ref, gram_ref,
    res_v, tiles_v, mid_v, own_v, mown_v, coarse_v, cb_v, basis_v, scale_v, x_v, fr_v,
    win1, win2, win3, oht, oh2t, ms_v, mrhs, mwin1, mwin2, mwin3, pair1, fx, ag, cw, dirb,
    ga, gd, dir_v, gram_v,
    lsem, dsem, hs, hr, es, er, msend, mrecv, psend, precv, fs, fr, ags, agr, bs, br, gs, gr,
):
    nb = tiles_v.shape[0]
    nm = mid_v.shape[0] - 2
    nch = ny * nz
    rows = 2 * nch
    cdev = coarse_v.shape[0]
    cols = res_v.shape[0]
    r = lax.axis_index("rows")
    x = lax.axis_index("cols")
    core = lax.rem(r, 2)
    chip = r // 2
    right = lax.rem(r + 1, rows)
    left = lax.rem(r + rows - 1, rows)
    partner = 2 * chip + 1 - core
    outer = lax.rem(r + 2 * core - 1 + rows, rows)
    outer2 = 2 * lax.rem(chip + 1 - 2 * core + nch, nch) + core
    step = nb // QUARTERS

    def remote(src, dst, ssem, rsem, where):
        return pltpu.make_async_remote_copy(
            src_ref=src, dst_ref=dst, send_sem=ssem, recv_sem=rsem,
            device_id=where, device_id_type=pl.DeviceIdType.MESH,
        )

    def local(src, dst, k):
        return pltpu.make_async_copy(src, dst, lsem.at[k])

    def lanes(g, n=1):
        return pl.ds(pl.multiple_of(g * L, L), n * L)

    pending = []

    def send(copy):
        copy.start()
        pending.append(copy)

    def pending_done():
        for copy in pending:
            copy.wait_send()

    def diag_in(q):
        at = pl.ds(q * step, step)
        return pltpu.make_async_copy(tiles_hbm.at[at, 0], tiles_v.at[at, 0], dsem.at[q])

    res_in = local(res_hbm, res_v, 1)
    off_in = local(tiles_hbm.at[:, 1:4], tiles_v.at[:, 1:4], 2)
    own_in = local(own_hbm, own_v, 3)
    mown_in = local(mown_hbm, mown_v, 4)
    mid_in = local(mid_hbm, mid_v.at[pl.ds(1, nm)], 5)
    coarse_in = local(coarse_hbm, coarse_v, 6)
    basis_in = local(basis_hbm, basis_v.at[x], 7)
    res_in.start()
    for q in range(QUARTERS):
        diag_in(q).start()
    for copy in (mid_in, own_in, mown_in, off_in, coarse_in, basis_in):
        copy.start()

    barrier = pltpu.get_barrier_semaphore()

    def greet(where):
        pl.semaphore_signal(
            barrier, inc=1, device_id=where, device_id_type=pl.DeviceIdType.MESH
        )

    greet({"rows": partner})
    greet({"rows": outer})

    @pl.loop(1, nch)
    def _(d):
        greet({"rows": 2 * lax.rem(chip + d, nch) + core})

    @pl.loop(1, nx)
    def _(d):
        greet({"cols": lax.rem(x + d, nx)})

    eye = lax.broadcasted_iota(jnp.int32, (L, L), 0) == lax.broadcasted_iota(
        jnp.int32, (L, L), 1
    )

    def weight(tile):
        d = jnp.sum(jnp.where(eye, tile.astype(F32), 0.0), axis=0, keepdims=True)
        return jnp.broadcast_to(W * (1.0 / d), (cols, L))

    def halo(win, k, lo, n):
        return (
            remote(win.at[pl.ds(nb + lo, n)], win.at[pl.ds(lo, n)], hs.at[k, 0], hr.at[k, 0], {"rows": right}),
            remote(win.at[pl.ds(nb + lo, n)], win.at[pl.ds(2 * nb + lo, n)], hs.at[k, 1], hr.at[k, 1], {"rows": left}),
        )

    def halo_start(win, k, lo, n):
        for copy in halo(win, k, lo, n):
            copy.start()
        if lo == 0:
            pending.extend(halo(win, k, 0, nb))

    def halo_wait(win, k):
        for copy in halo(win, k, 0, nb):
            copy.wait_recv()

    def first(g, carry):
        s = weight(tiles_v[g, 0])
        scale_v[g] = s
        win1[nb + g] = (s * res_v[:, lanes(g)]).astype(BF)
        return carry

    res_in.wait()
    for q in range(QUARTERS):
        diag_in(q).wait()
        lax.fori_loop(q * step, (q + 1) * step, first, 0, unroll=min(8, step))
        if q == 0:
            pl.semaphore_wait(barrier, nch - 1 + 2 + nx - 1)
        halo_start(win1, 0, q * step, step)

    basis_in.wait()

    def basis_copy(d):
        return remote(
            basis_v.at[x], basis_v.at[x], bs, br, {"cols": lax.rem(x + d, nx)}
        )

    @pl.loop(1, nx)
    def _(d):
        basis_copy(d).start()

    basis_all = remote(
        basis_v.at[pl.ds(0, nx - 1)], basis_v.at[pl.ds(0, nx - 1)], bs, br,
        {"rows": partner},
    )
    pending.append(basis_all)

    mid_in.wait()
    mown_in.wait()
    wide_iota = lax.broadcasted_iota(jnp.int32, (2 * cdev, L), 0)
    mid_base = (r - core) * cdev
    for g in range(nm):
        oh2t[1 + g] = jnp.where(
            wide_iota == mown_v[g : g + 1, :] - mid_base, 1.0, 0.0
        ).astype(BF)
        ms_v[2 + g] = weight(mid_v[1 + g, 1])
    edges = []
    for k, (buf, n, lo, hi) in enumerate(((mid_v, 1, 1, nm), (oh2t, 1, 1, nm), (ms_v, 2, 2, nm))):
        edges.append(
            remote(buf.at[pl.ds(hi, n)], buf.at[pl.ds(0, n)], es.at[k, 0], er.at[k, 0], {"rows": right})
        )
        edges.append(
            remote(buf.at[pl.ds(lo, n)], buf.at[pl.ds(lo + nm, n)], es.at[k, 1], er.at[k, 1], {"rows": left})
        )
    for copy in edges:
        send(copy)

    own_in.wait()
    low_iota = lax.broadcasted_iota(jnp.int32, (L, L), 0)
    fine_base = r * (nm * L)

    def owner_row(g):
        return own_v[pl.ds(g, 1), :] - fine_base

    def hot(g, carry):
        low = jnp.bitwise_and(owner_row(g), L - 1)
        oht[:, lanes(g)] = jnp.where(low_iota == low, 1.0, 0.0).astype(BF)
        return carry

    lax.fori_loop(0, nb, hot, 0, unroll=4)

    off_in.wait()
    halo_wait(win1, 0)
    base = (r - 1) * nb

    def product(win, g):
        picked = [win[nb + g]] + [
            win[jnp.clip(idx_ref[s, g] - base, 0, 3 * nb - 1)] for s in (1, 2, 3)
        ]
        tile = [tiles_v[g, s] for s in range(4)]
        return dot(jnp.concatenate(picked, axis=1), jnp.concatenate(tile, axis=1), NT)

    def fine_b(g, carry):
        s = scale_v[g]
        rhs = res_v[:, lanes(g)]
        v = s * rhs + s * (rhs - product(win1, g))
        x_v[g] = v
        win2[nb + g] = v.astype(BF)
        return carry

    for q in range(QUARTERS):
        lax.fori_loop(q * step, (q + 1) * step, fine_b, 0, unroll=step)
        halo_start(win2, 1, q * step, step)

    coarse_in.wait()

    def convert(c, carry):
        for k in range(2):
            at = pl.multiple_of((2 * c + k) * cdev, cdev)
            cb_v[k, c] = coarse_v[:, pl.ds(at, cdev)].astype(BF)
        return carry

    lax.fori_loop(0, nch, convert, 0, unroll=2)
    halo_wait(win2, 1)

    def residual(g, carry):
        fr_v[g] = res_v[:, lanes(g)] - product(win2, g)
        return carry

    lax.fori_loop(0, nb, residual, 0, unroll=min(32, nb))

    def restrict(c, acc):
        parts = []
        for k in range(4):
            g = 4 * c + k
            high = jnp.broadcast_to(lax.shift_right_logical(owner_row(g), 7), (cols, L))
            v = fr_v[g]
            parts.append(
                jnp.concatenate(
                    [jnp.where(high == h, v, 0.0).astype(BF) for h in range(nm)], axis=0
                )
            )
        return acc + dot(jnp.concatenate(parts, axis=1), oht[:, lanes(4 * c, 4)], NT)

    mid_rhs = lax.fori_loop(
        0, nb // 4, restrict, jnp.zeros((nm * cols, L), F32), unroll=nb // 4
    ).reshape(nm, cols, L)

    mrhs[2 : nm + 2] = mid_rhs
    rhs_edges = (
        remote(mrhs.at[pl.ds(nm, 2)], mrhs.at[pl.ds(0, 2)], msend.at[0], mrecv.at[0], {"rows": right}),
        remote(mrhs.at[pl.ds(2, 2)], mrhs.at[pl.ds(nm + 2, 2)], msend.at[1], mrecv.at[1], {"rows": left}),
    )
    for copy in rhs_edges:
        send(copy)

    def inside(v, left_side):
        keep = r > 0 if left_side else r < rows - 1
        return jnp.where(keep, v, jnp.zeros_like(v))

    def mid_product(mwin, g, before):
        v3 = jnp.concatenate([mwin[before + k] for k in range(3)], axis=1)
        t3 = jnp.concatenate([mid_v[g, k] for k in range(3)], axis=1)
        return dot(v3, t3, NT)

    mb = [None] * (nm + 2)

    def mid_b(g):
        s = ms_v[g + 1]
        rhs = mrhs[g + 1]
        mb[g] = s * rhs + s * (rhs - mid_product(mwin1, g, g))

    for g in range(2, nm + 2):
        mwin1[g] = (ms_v[g] * mrhs[g]).astype(BF)
    for g in range(2, nm):
        mid_b(g)
    for copy in edges:
        copy.wait_recv()
    for copy in rhs_edges:
        copy.wait_recv()
    for g in (0, 1, nm + 2, nm + 3):
        mwin1[g] = inside(ms_v[g] * mrhs[g], g < 2).astype(BF)
    for g in (0, 1, nm, nm + 1):
        mid_b(g)
    for g in range(nm + 2):
        v = mb[g]
        if g in (0, nm + 1):
            v = inside(v, g == 0)
        mwin2[g] = v.astype(BF)
    mid_res = [mrhs[g + 1] - mid_product(mwin2, g, g - 1) for g in range(1, nm + 1)]

    flat = jnp.concatenate(mid_res, axis=1)
    hot2 = jnp.concatenate([oh2t[1 + g] for g in range(nm)], axis=1)
    both = dot(jnp.concatenate(split(flat), axis=0), hot2, NT)
    partial = both[:cols] + both[cols:]
    even, odd = partial[:, :cdev], partial[:, cdev:]
    pair1[0] = jnp.where(core == 0, odd, even)
    swap1 = remote(pair1.at[0], pair1.at[1], psend.at[0], precv.at[0], {"rows": partner})
    send(swap1)
    swap1.wait_recv()
    coarse_rhs = jnp.where(core == 0, even, odd) + pair1[1]

    ag[core, chip] = coarse_rhs.astype(BF)

    def ag_copy(d):
        return remote(
            ag.at[core, chip], ag.at[core, chip], ags.at[0], agr.at[0],
            {"rows": 2 * lax.rem(chip + d, nch) + core},
        )

    @pl.loop(1, nch)
    def _(d):
        ag_copy(d).start()

    ag_all = remote(
        ag.at[core, pl.ds(0, nch - 1)], ag.at[core, pl.ds(0, nch - 1)],
        ags.at[0], agr.at[0], {"rows": partner},
    )
    pending.append(ag_all)
    ag_all.wait_recv()
    half = remote(ag.at[core], ag.at[core], ags.at[1], agr.at[1], {"rows": partner})
    send(half)

    def coarse_half(k, acc):
        def chunk(c, acc):
            v = jnp.concatenate([ag[k, 4 * c + i] for i in range(4)], axis=1)
            t = jnp.concatenate([cb_v[k, 4 * c + i] for i in range(4)], axis=1)
            return acc + dot(v, t, NT)

        return lax.fori_loop(0, nch // 4, chunk, acc, unroll=nch // 4)

    fix = coarse_half(core, jnp.zeros((cols, cdev), F32))
    half.wait_recv()
    fix = coarse_half(1 - core, fix)

    fx[0] = fix
    fix_out = [
        remote(fx.at[0], fx.at[1 + k], fs.at[k], fr.at[k], {"rows": to})
        for k, to in enumerate((partner, outer, outer2))
    ]
    for copy in fix_out:
        send(copy)

    def halves(a, b):
        return jnp.concatenate([jnp.where(core == 0, a, b), jnp.where(core == 0, b, a)], axis=1)

    def lifted(values, hots):
        both = dot(jnp.concatenate(split(values), axis=0), hots, NN)
        return both[:cols] + both[cols:]

    def mid_c(g, lift):
        mb[g] = mb[g] + lift
        v = mb[g]
        if g in (0, nm + 1):
            v = inside(v, g == 0)
        mwin3[g] = v.astype(BF)

    def mid_d(g):
        mb[g] = mb[g] + ms_v[g + 1] * (mrhs[g + 1] - mid_product(mwin3, g, g - 1))

    fix_out[0].wait_recv()
    pair = halves(fix, fx[1])
    lift = lifted(pair, hot2)
    for g in range(1, nm + 1):
        mid_c(g, lift[:, (g - 1) * L : g * L])
    for g in range(2, nm):
        mid_d(g)
    for copy in fix_out[1:]:
        copy.wait_recv()
    pair2 = halves(fx[3], fx[2])
    mid_c(0, lifted(jnp.where(core == 0, pair2, pair), oh2t[0]))
    mid_c(nm + 1, lifted(jnp.where(core == 0, pair, pair2), oh2t[nm + 1]))
    mid_d(1)
    mid_d(nm)

    md = jnp.concatenate(mb[1 : nm + 1], axis=0)
    cw[...] = jnp.concatenate(split(md), axis=1)

    wide = min(8, step)

    def prolong(c, carry):
        hots = oht[:, lanes(wide * c, wide)]
        up = dot(cw[...], jnp.concatenate([hots, hots], axis=0), NN)
        for k in range(wide):
            g = wide * c + k
            high = jnp.broadcast_to(lax.shift_right_logical(owner_row(g), 7), (cols, L))
            v = x_v[g]
            for h in range(nm):
                v = v + jnp.where(
                    high == h, up[h * cols : (h + 1) * cols, k * L : (k + 1) * L], 0.0
                )
            x_v[g] = v
            win3[nb + g] = v.astype(BF)
        return carry

    each = step // wide
    for q in range(QUARTERS):
        lax.fori_loop(q * each, (q + 1) * each, prolong, 0, unroll=each)
        halo_start(win3, 2, q * step, step)
    halo_wait(win3, 2)

    def finish(g, carry):
        v = x_v[g] + scale_v[g] * (res_v[:, lanes(g)] - product(win3, g))
        dir_v[:, lanes(g)] = v
        dirb[:, lanes(g)] = v.astype(BF)
        return carry

    def dir_out(q):
        at = pl.ds(q * (nb // 2) * L, (nb // 2) * L)
        return pltpu.make_async_copy(dir_v.at[:, at], dir_ref.at[:, at], dsem.at[q])

    for q in range(2):
        lax.fori_loop(q * (nb // 2), (q + 1) * (nb // 2), finish, 0, unroll=nb // 2)
        dir_out(q).start()

    basis_all.wait_recv()

    def gram(c, acc):
        t = basis_v[:, :, lanes(4 * c, 4)].reshape(nx * cols, 4 * L)
        return acc + dot(dirb[:, lanes(4 * c, 4)], t, NT)

    total = lax.fori_loop(
        0, nb // 4, gram, jnp.zeros((cols, nx * cols), F32), unroll=nb // 4
    )
    rows8 = cols // 2
    ga[core] = jnp.concatenate([total[:rows8], total[rows8:]], axis=1)
    swap3 = remote(ga.at[core], ga.at[core], gs.at[0], gr.at[0], {"rows": partner})
    send(swap3)
    swap3.wait_recv()
    gd[chip] = ga[0] + ga[1]

    @pl.loop(1, nch)
    def _(d):
        to = 2 * lax.rem(chip + d, nch) + core
        remote(gd.at[chip], gd.at[chip], gs.at[1], gr.at[1], {"rows": to}).start()

    gd_all = remote(
        gd.at[pl.ds(0, nch - 1)], gd.at[pl.ds(0, nch - 1)], gs.at[1], gr.at[1], {"rows": partner}
    )
    pending.append(gd_all)
    gd_all.wait_recv()
    parts = [gd[k] for k in range(nch)]
    while len(parts) > 1:
        parts = [a + b for a, b in zip(parts[::2], parts[1::2])]
    acc = parts[0]
    wide = nx * cols
    gram_v[...] = jnp.concatenate([acc[:, :wide], acc[:, wide:]], axis=0)
    gram_out = local(gram_v, gram_ref, 0)
    gram_out.start()
    dir_out(0).wait()
    dir_out(1).wait()
    gram_out.wait()
    pending_done()


def place(a_ref, b_ref, a_out, b_out, sem):
    copies = [
        pltpu.make_async_copy(a_ref, a_out, sem.at[0]),
        pltpu.make_async_copy(b_ref, b_out, sem.at[1]),
    ]
    for copy in copies:
        copy.start()
    for copy in copies:
        copy.wait()


def on_device(ny, nz, nx, residual, basis, fine_tiles, fine_index, mid_tiles, fine_owner, mid_owner, coarse):
    nb = fine_tiles.shape[0]
    nm = mid_tiles.shape[0]
    cols = residual.shape[1]
    cdev = coarse.shape[0]
    n = nb * L
    nch = ny * nz
    vm, dma = pltpu.VMEM, pltpu.SemaphoreType.DMA
    scratch = [
        vm((cols, n), F32), vm((nb, 4, L, L), BF), vm((nm + 2, 3, L, L), BF),
        vm((nb, L), jnp.int32), vm((nm, L), jnp.int32),
        vm(coarse.shape, F32), vm((2, nch, cdev, cdev), BF), vm((nx, cols, n), BF),
        vm((nb, cols, L), F32), vm((nb, cols, L), F32), vm((nb, cols, L), F32),
        vm((3 * nb, cols, L), BF), vm((3 * nb, cols, L), BF), vm((3 * nb, cols, L), BF),
        vm((L, n), BF), vm((nm + 2, 2 * cdev, L), BF), vm((nm + 4, cols, L), F32),
        vm((nm + 4, cols, L), F32),
        vm((nm + 4, cols, L), BF), vm((nm + 2, cols, L), BF), vm((nm + 2, cols, L), BF),
        vm((2, cols, cdev), F32), vm((4, cols, cdev), F32), vm((2, nch, cols, cdev), BF),
        vm((nm * cols, 2 * L), BF), vm((cols, n), BF),
        vm((2, cols // 2, 2 * nx * cols), F32), vm((nch, cols // 2, 2 * nx * cols), F32),
        vm((cols, n), F32), vm((cols, nx * cols), F32),
        dma((8,)), dma((QUARTERS,)), dma((3, 2)), dma((3, 2)), dma((3, 2)), dma((3, 2)),
        dma((2,)), dma((2,)), dma((1,)), dma((1,)), dma((3,)), dma((3,)),
        dma((2,)), dma((2,)), dma, dma, dma((2,)), dma((2,)),
    ]
    hbm = pl.BlockSpec(memory_space=pl.ANY)
    directions, gram = pl.pallas_call(
        functools.partial(kernel, ny, nz, nx),
        out_shape=(
            jax.ShapeDtypeStruct((cols, n), F32),
            jax.ShapeDtypeStruct((cols, nx * cols), F32),
        ),
        in_specs=[hbm, hbm, hbm, pl.BlockSpec(memory_space=pltpu.SMEM), hbm, hbm, hbm, hbm],
        out_specs=(hbm, hbm),
        scratch_shapes=scratch,
        name="vcycle",
        compiler_params=pltpu.CompilerParams(
            collective_id=0, has_side_effects=True, vmem_limit_bytes=56 * 2**20
        ),
    )(
        residual.T, basis.T, fine_tiles, fine_index.T, mid_tiles,
        fine_owner.reshape(nb, L), mid_owner.reshape(nm, L), coarse,
    )
    directions, gram = pl.pallas_call(
        place,
        out_shape=(
            jax.ShapeDtypeStruct((cols, n), F32),
            jax.ShapeDtypeStruct((cols, nx * cols), F32),
        ),
        in_specs=[hbm, hbm],
        out_specs=(hbm, hbm),
        scratch_shapes=[dma((2,))],
        name="place",
    )(directions, gram)
    return directions.T, gram.T


def solution(mesh, ny=4, nz=8):
    in_specs = (
        P("rows", "cols"),
        P("rows", "cols"),
        P("rows", None, None, None),
        P("rows", None),
        P("rows", None, None, None),
        P("rows"),
        P("rows"),
        P("rows", None),
    )
    out_specs = (P("rows", "cols"), P(None, "cols"))
    return jax.shard_map(
        functools.partial(on_device, ny, nz, mesh.shape["cols"]),
        mesh=mesh, in_specs=in_specs, out_specs=out_specs, check_vma=False,
    )
```

time: 74.8 us -> 79.7 us (1.066)
  Pallas kernels: 70.8 us -> 78.9 us
  local copies, waits for them, and re-layouts: 3.16 us -> 0 us
    pallas_call x0 -> x1, Pallas kernels: none -> 17.3 us  [on_device(): pl.pallas_call(place, out_shape=(jax.ShapeDtypeStruct((cols, n), F32), ja...]
    pallas_call x1, Pallas kernels: 70.8 us -> 61.7 us  [on_device(): pl.pallas_call(functools.partial(kernel, ny, nz, nx), out_shape=(jax.Shap...]
    unnamed x2 -> x0, local copies, waits for them, and re-layouts: 3.16 us -> none
where the time goes in v2:
time: 79.7 us; the launch traced here: 79.5 us
  Pallas kernels  78.9 us (99%)
    pallas_call x1, Pallas kernels, on_device(): pl.pallas_call(functools.partial(kernel, ny, nz, nx), out_shape=(jax.Shap...  61.7 us
    pallas_call x1, Pallas kernels, on_device(): pl.pallas_call(place, out_shape=(jax.ShapeDtypeStruct((cols, n), F32), ja...  17.3 us

profile of v2, /device:TPU:1, one launch (start us, length us, event | category | flops | bytes accessed | tf_op | source)
XLA Modules:
  0.0 79.5 jit_solution(10888953682074788352)
XLA Ops:
  0.6 61.7 %vcycle.1 = (f32[16,8192]{1,0:T(8,128)}, f32[16,64]{1,0:T(8,128)}) custom-call(f32[16,8192]{1,0:T(8,128)} %bitcast.7, bf16[16,8192]{1,0:T(8,128)(2,1)} %bitcast.8, bf16[64,4,128,128]{3,2,1,0:T(8,128)(2,1)} %tiles_hbm.1, s32[4,64]{1,0:T(4,128)} %bitcast.11, bf16[8,3,128,128]{3,2,1,0:T(8,128)(2,1)} %mid_hbm.1, s32[64,128]{1,0:T(8,128)} %bitcast.9, ...), custom_call_target="tpu_custom_call" | custom-call | tf_op jit(solution)/shard_map/vcycle/pallas_call | solution.py:501
  62.3 17.3 %place.1 = (f32[16,8192]{1,0:T(8,128)}, f32[16,64]{1,0:T(8,128)}) custom-call(f32[16,8192]{1,0:T(8,128)} %get-tuple-element.6.a_ref, f32[16,64]{1,0:T(8,128)} %get-tuple-element.7.b_ref), custom_call_target="tpu_custom_call" | custom-call | tf_op jit(solution)/shard_map/place/pallas_call | solution.py:518

commit v3 on v2

--- a/solution.py
+++ b/solution.py
@@ -461,15 +461,9 @@
     pending_done()
 
 
-def place(a_ref, b_ref, a_out, b_out, sem):
-    copies = [
-        pltpu.make_async_copy(a_ref, a_out, sem.at[0]),
-        pltpu.make_async_copy(b_ref, b_out, sem.at[1]),
-    ]
-    for copy in copies:
-        copy.start()
-    for copy in copies:
-        copy.wait()
+def place(a_ref, b_ref, a_out, b_out):
+    a_out[...] = a_ref[...]
+    b_out[...] = b_ref[...]
 
 
 def on_device(ny, nz, nx, residual, basis, fine_tiles, fine_index, mid_tiles, fine_owner, mid_owner, coarse):
@@ -521,9 +515,9 @@
             jax.ShapeDtypeStruct((cols, n), F32),
             jax.ShapeDtypeStruct((cols, nx * cols), F32),
         ),
-        in_specs=[hbm, hbm],
-        out_specs=(hbm, hbm),
-        scratch_shapes=[dma((2,))],
+        grid=(2,),
+        in_specs=[pl.BlockSpec((cols, n // 2), lambda i: (0, i)), pl.BlockSpec((cols, nx * cols), lambda i: (0, 0))],
+        out_specs=(pl.BlockSpec((cols, n // 2), lambda i: (0, i)), pl.BlockSpec((cols, nx * cols), lambda i: (0, 0))),
         name="place",
     )(directions, gram)
     return directions.T, gram.T

time: 79.7 us -> 64.2 us (0.81)
  Pallas kernels: 78.9 us -> 63.4 us
    pallas_call x1, Pallas kernels: 17.3 us -> 1.79 us  [on_device(): pl.pallas_call(place, out_shape=(jax.ShapeDtypeStruct((cols, n), F32), ja...]
where the time goes in v3:
time: 64.2 us; the launch traced here: 64.1 us
  Pallas kernels  63.4 us (99%)
    pallas_call x1, Pallas kernels, on_device(): pl.pallas_call(functools.partial(kernel, ny, nz, nx), out_shape=(jax.Shap...  61.7 us
    pallas_call x1, Pallas kernels, on_device(): pl.pallas_call(place, out_shape=(jax.ShapeDtypeStruct((cols, n), F32), ja...  1.79 us

profile of v3, /device:TPU:1, one launch (start us, length us, event | category | flops | bytes accessed | tf_op | source)
XLA Modules:
  0.0 64.1 jit_solution(1466479919380345083)
XLA Ops:
  0.6 61.7 %vcycle.1 = (f32[16,8192]{1,0:T(8,128)}, f32[16,64]{1,0:T(8,128)}) custom-call(f32[16,8192]{1,0:T(8,128)} %bitcast.7, bf16[16,8192]{1,0:T(8,128)(2,1)} %bitcast.8, bf16[64,4,128,128]{3,2,1,0:T(8,128)(2,1)} %tiles_hbm.1, s32[4,64]{1,0:T(4,128)} %bitcast.11, bf16[8,3,128,128]{3,2,1,0:T(8,128)(2,1)} %mid_hbm.1, s32[64,128]{1,0:T(8,128)} %bitcast.9, ...), custom_call_target="tpu_custom_call" | custom-call | tf_op jit(solution)/shard_map/vcycle/pallas_call | solution.py:495
  62.3 1.8 %place.1 = (f32[16,8192]{1,0:T(8,128)}, f32[16,64]{1,0:T(8,128)}) custom-call(f32[16,8192]{1,0:T(8,128)} %get-tuple-element.6.a_ref, f32[16,64]{1,0:T(8,128)} %get-tuple-element.7.b_ref), custom_call_target="tpu_custom_call" | custom-call | tf_op jit(solution)/shard_map/place/pallas_call | solution.py:512

commit v4 on v3

--- a/solution.py
+++ b/solution.py
@@ -44,8 +44,6 @@
     x = lax.axis_index("cols")
     core = lax.rem(r, 2)
     chip = r // 2
-    right = lax.rem(r + 1, rows)
-    left = lax.rem(r + rows - 1, rows)
     partner = 2 * chip + 1 - core
     outer = lax.rem(r + 2 * core - 1 + rows, rows)
     outer2 = 2 * lax.rem(chip + 1 - 2 * core + nch, nch) + core
@@ -64,14 +62,24 @@
         return pl.ds(pl.multiple_of(g * L, L), n * L)
 
     pending = []
-
-    def send(copy):
-        copy.start()
-        pending.append(copy)
+    bordered = jnp.logical_and(r > 0, r < rows - 1)
+
+    def guarded(when, act):
+        if when is None:
+            act()
+        else:
+            pl.when(when)(act)
+
+    def send(copy, when=None):
+        guarded(when, copy.start)
+        pending.append((copy, when))
+
+    def received(copy, when=None):
+        guarded(when, copy.wait_recv)
 
     def pending_done():
-        for copy in pending:
-            copy.wait_send()
+        for copy, when in pending:
+            guarded(when, copy.wait_send)
 
     def diag_in(q):
         at = pl.ds(q * step, step)
@@ -116,21 +124,35 @@
         d = jnp.sum(jnp.where(eye, tile.astype(F32), 0.0), axis=0, keepdims=True)
         return jnp.broadcast_to(W * (1.0 / d), (cols, L))
 
+    far_part = 2 * nb * (1 - core)
+    near_part = 2 * nb * core
+
     def halo(win, k, lo, n):
+        own = win.at[pl.ds(nb + lo, n)]
         return (
-            remote(win.at[pl.ds(nb + lo, n)], win.at[pl.ds(lo, n)], hs.at[k, 0], hr.at[k, 0], {"rows": right}),
-            remote(win.at[pl.ds(nb + lo, n)], win.at[pl.ds(2 * nb + lo, n)], hs.at[k, 1], hr.at[k, 1], {"rows": left}),
+            (remote(own, win.at[pl.ds(far_part + lo, n)], hs.at[k, 0], hr.at[k, 0], {"rows": outer}), bordered),
+            (remote(own, win.at[pl.ds(near_part + lo, n)], hs.at[k, 1], hr.at[k, 1], {"rows": partner}), None),
         )
 
     def halo_start(win, k, lo, n):
-        for copy in halo(win, k, lo, n):
-            copy.start()
+        for copy, when in halo(win, k, lo, n):
+            guarded(when, copy.start)
         if lo == 0:
             pending.extend(halo(win, k, 0, nb))
 
     def halo_wait(win, k):
-        for copy in halo(win, k, 0, nb):
-            copy.wait_recv()
+        for copy, when in halo(win, k, 0, nb):
+            received(copy, when)
+
+    yc = chip // nz
+    zc = lax.rem(chip, nz)
+    steps = sorted(
+        ((dy, dz) for dy in range(ny) for dz in range(nz) if dy or dz),
+        key=lambda d: -min(d[0], ny - d[0]) - min(d[1], nz - d[1]),
+    )
+
+    def chip_at(dy, dz):
+        return lax.rem(yc + dy, ny) * nz + lax.rem(zc + dz, nz)
 
     def first(g, carry):
         s = weight(tiles_v[g, 0])
@@ -161,7 +183,7 @@
         basis_v.at[pl.ds(0, nx - 1)], basis_v.at[pl.ds(0, nx - 1)], bs, br,
         {"rows": partner},
     )
-    pending.append(basis_all)
+    pending.append((basis_all, None))
 
     mid_in.wait()
     mown_in.wait()
@@ -172,16 +194,22 @@
             wide_iota == mown_v[g : g + 1, :] - mid_base, 1.0, 0.0
         ).astype(BF)
         ms_v[2 + g] = weight(mid_v[1 + g, 1])
+
+    def edge_copies(buf, n, own, ssem, rsem):
+        out_at = own + core * (nm - n)
+        out_to = own + nm - core * (nm + n)
+        in_at = own + (1 - core) * (nm - n)
+        in_to = own - n + core * (nm + n)
+        return (
+            (remote(buf.at[pl.ds(out_at, n)], buf.at[pl.ds(out_to, n)], ssem.at[0], rsem.at[0], {"rows": outer}), bordered),
+            (remote(buf.at[pl.ds(in_at, n)], buf.at[pl.ds(in_to, n)], ssem.at[1], rsem.at[1], {"rows": partner}), None),
+        )
+
     edges = []
-    for k, (buf, n, lo, hi) in enumerate(((mid_v, 1, 1, nm), (oh2t, 1, 1, nm), (ms_v, 2, 2, nm))):
-        edges.append(
-            remote(buf.at[pl.ds(hi, n)], buf.at[pl.ds(0, n)], es.at[k, 0], er.at[k, 0], {"rows": right})
-        )
-        edges.append(
-            remote(buf.at[pl.ds(lo, n)], buf.at[pl.ds(lo + nm, n)], es.at[k, 1], er.at[k, 1], {"rows": left})
-        )
-    for copy in edges:
-        send(copy)
+    for k, (buf, n, own) in enumerate(((mid_v, 1, 1), (oh2t, 1, 1), (ms_v, 2, 2))):
+        edges.extend(edge_copies(buf, n, own, es.at[k], er.at[k]))
+    for copy, when in edges:
+        send(copy, when)
 
     own_in.wait()
     low_iota = lax.broadcasted_iota(jnp.int32, (L, L), 0)
@@ -255,12 +283,9 @@
     ).reshape(nm, cols, L)
 
     mrhs[2 : nm + 2] = mid_rhs
-    rhs_edges = (
-        remote(mrhs.at[pl.ds(nm, 2)], mrhs.at[pl.ds(0, 2)], msend.at[0], mrecv.at[0], {"rows": right}),
-        remote(mrhs.at[pl.ds(2, 2)], mrhs.at[pl.ds(nm + 2, 2)], msend.at[1], mrecv.at[1], {"rows": left}),
-    )
-    for copy in rhs_edges:
-        send(copy)
+    rhs_edges = edge_copies(mrhs, 2, 2, msend, mrecv)
+    for copy, when in rhs_edges:
+        send(copy, when)
 
     def inside(v, left_side):
         keep = r > 0 if left_side else r < rows - 1
@@ -282,10 +307,8 @@
         mwin1[g] = (ms_v[g] * mrhs[g]).astype(BF)
     for g in range(2, nm):
         mid_b(g)
-    for copy in edges:
-        copy.wait_recv()
-    for copy in rhs_edges:
-        copy.wait_recv()
+    for copy, when in (*edges, *rhs_edges):
+        received(copy, when)
     for g in (0, 1, nm + 2, nm + 3):
         mwin1[g] = inside(ms_v[g] * mrhs[g], g < 2).astype(BF)
     for g in (0, 1, nm, nm + 1):
@@ -310,21 +333,15 @@
 
     ag[core, chip] = coarse_rhs.astype(BF)
 
-    def ag_copy(d):
-        return remote(
-            ag.at[core, chip], ag.at[core, chip], ags.at[0], agr.at[0],
-            {"rows": 2 * lax.rem(chip + d, nch) + core},
-        )
-
-    @pl.loop(1, nch)
-    def _(d):
-        ag_copy(d).start()
+    for d in steps:
+        to = 2 * chip_at(*d) + core
+        remote(ag.at[core, chip], ag.at[core, chip], ags.at[0], agr.at[0], {"rows": to}).start()
 
     ag_all = remote(
         ag.at[core, pl.ds(0, nch - 1)], ag.at[core, pl.ds(0, nch - 1)],
         ags.at[0], agr.at[0], {"rows": partner},
     )
-    pending.append(ag_all)
+    pending.append((ag_all, None))
     ag_all.wait_recv()
     half = remote(ag.at[core], ag.at[core], ags.at[1], agr.at[1], {"rows": partner})
     send(half)
@@ -346,8 +363,9 @@
         remote(fx.at[0], fx.at[1 + k], fs.at[k], fr.at[k], {"rows": to})
         for k, to in enumerate((partner, outer, outer2))
     ]
-    for copy in fix_out:
-        send(copy)
+    last_but = jnp.logical_and(r != 1, r != rows - 2)
+    for copy, when in zip(fix_out[::-1], (last_but, bordered, None)):
+        send(copy, when)
 
     def halves(a, b):
         return jnp.concatenate([jnp.where(core == 0, a, b), jnp.where(core == 0, b, a)], axis=1)
@@ -374,7 +392,7 @@
     for g in range(2, nm):
         mid_d(g)
     for copy in fix_out[1:]:
-        copy.wait_recv()
+        received(copy, bordered)
     pair2 = halves(fx[3], fx[2])
     mid_c(0, lifted(jnp.where(core == 0, pair2, pair), oh2t[0]))
     mid_c(nm + 1, lifted(jnp.where(core == 0, pair, pair2), oh2t[nm + 1]))
@@ -437,15 +455,14 @@
     swap3.wait_recv()
     gd[chip] = ga[0] + ga[1]
 
-    @pl.loop(1, nch)
-    def _(d):
-        to = 2 * lax.rem(chip + d, nch) + core
+    for d in steps:
+        to = 2 * chip_at(*d) + core
         remote(gd.at[chip], gd.at[chip], gs.at[1], gr.at[1], {"rows": to}).start()
 
     gd_all = remote(
         gd.at[pl.ds(0, nch - 1)], gd.at[pl.ds(0, nch - 1)], gs.at[1], gr.at[1], {"rows": partner}
     )
-    pending.append(gd_all)
+    pending.append((gd_all, None))
     gd_all.wait_recv()
     parts = [gd[k] for k in range(nch)]
     while len(parts) > 1:

time: 64.2 us -> 62.1 us (0.967); the launches traced: 64.1 us -> 61.2 us
  Pallas kernels: 63.4 us -> 60.6 us
    pallas_call x1, Pallas kernels: 61.7 us -> 58.8 us  [on_device(): pl.pallas_call(functools.partial(kernel, ny, nz, nx), out_shape=(jax.Shap...]
where the time goes in v4:
time: 62.1 us; the launch traced here: 61.2 us
  Pallas kernels  60.6 us (98%)
  between operations  0.64 us (1%)
    pallas_call x1, Pallas kernels, on_device(): pl.pallas_call(functools.partial(kernel, ny, nz, nx), out_shape=(jax.Shap...  58.8 us
    pallas_call x1, Pallas kernels, on_device(): pl.pallas_call(place, out_shape=(jax.ShapeDtypeStruct((cols, n), F32), ja...  1.79 us

profile of v4, /device:TPU:1, one launch (start us, length us, event | category | flops | bytes accessed | tf_op | source)
XLA Modules:
  0.0 61.2 jit_solution(15486068154573487320)
XLA Ops:
  0.6 58.8 %vcycle.1 = (f32[16,8192]{1,0:T(8,128)}, f32[16,64]{1,0:T(8,128)}) custom-call(f32[16,8192]{1,0:T(8,128)} %bitcast.7, bf16[16,8192]{1,0:T(8,128)(2,1)} %bitcast.8, bf16[64,4,128,128]{3,2,1,0:T(8,128)(2,1)} %tiles_hbm.1, s32[4,64]{1,0:T(4,128)} %bitcast.11, bf16[8,3,128,128]{3,2,1,0:T(8,128)(2,1)} %mid_hbm.1, s32[64,128]{1,0:T(8,128)} %bitcast.9, ...), custom_call_target="tpu_custom_call" | custom-call | tf_op jit(solution)/shard_map/vcycle/pallas_call | solution.py:512
  59.5 1.8 %place.1 = (f32[16,8192]{1,0:T(8,128)}, f32[16,64]{1,0:T(8,128)}) custom-call(f32[16,8192]{1,0:T(8,128)} %get-tuple-element.6.a_ref, f32[16,64]{1,0:T(8,128)} %get-tuple-element.7.b_ref), custom_call_target="tpu_custom_call" | custom-call | tf_op jit(solution)/shard_map/place/pallas_call | solution.py:529

commit v5 on v4

--- a/solution.py
+++ b/solution.py
@@ -92,29 +92,29 @@
     mid_in = local(mid_hbm, mid_v.at[pl.ds(1, nm)], 5)
     coarse_in = local(coarse_hbm, coarse_v, 6)
     basis_in = local(basis_hbm, basis_v.at[x], 7)
+    barrier = pltpu.get_barrier_semaphore()
+
+    def greet(where):
+        pl.semaphore_signal(
+            barrier, inc=1, device_id=where, device_id_type=pl.DeviceIdType.MESH
+        )
+
+    greet({"rows": partner})
+    greet({"rows": outer})
+
+    @pl.loop(1, nch)
+    def _(d):
+        greet({"rows": 2 * lax.rem(chip + d, nch) + core})
+
+    @pl.loop(1, nx)
+    def _(d):
+        greet({"cols": lax.rem(x + d, nx)})
+
     res_in.start()
     for q in range(QUARTERS):
         diag_in(q).start()
     for copy in (mid_in, own_in, mown_in, off_in, coarse_in, basis_in):
         copy.start()
-
-    barrier = pltpu.get_barrier_semaphore()
-
-    def greet(where):
-        pl.semaphore_signal(
-            barrier, inc=1, device_id=where, device_id_type=pl.DeviceIdType.MESH
-        )
-
-    greet({"rows": partner})
-    greet({"rows": outer})
-
-    @pl.loop(1, nch)
-    def _(d):
-        greet({"rows": 2 * lax.rem(chip + d, nch) + core})
-
-    @pl.loop(1, nx)
-    def _(d):
-        greet({"cols": lax.rem(x + d, nx)})
 
     eye = lax.broadcasted_iota(jnp.int32, (L, L), 0) == lax.broadcasted_iota(
         jnp.int32, (L, L), 1
@@ -194,6 +194,8 @@
             wide_iota == mown_v[g : g + 1, :] - mid_base, 1.0, 0.0
         ).astype(BF)
         ms_v[2 + g] = weight(mid_v[1 + g, 1])
+        for k in range(3):
+            mid_v[1 + g, k] = mid_v[1 + g, k].T
 
     def edge_copies(buf, n, own, ssem, rsem):
         out_at = own + core * (nm - n)
@@ -226,6 +228,13 @@
     lax.fori_loop(0, nb, hot, 0, unroll=4)
 
     off_in.wait()
+
+    def turn(g, carry):
+        for s in range(4):
+            tiles_v[g, s] = tiles_v[g, s].T
+        return carry
+
+    lax.fori_loop(0, nb, turn, 0, unroll=min(16, nb))
     halo_wait(win1, 0)
     base = (r - 1) * nb
 
@@ -234,7 +243,7 @@
             win[jnp.clip(idx_ref[s, g] - base, 0, 3 * nb - 1)] for s in (1, 2, 3)
         ]
         tile = [tiles_v[g, s] for s in range(4)]
-        return dot(jnp.concatenate(picked, axis=1), jnp.concatenate(tile, axis=1), NT)
+        return dot(jnp.concatenate(picked, axis=1), jnp.concatenate(tile, axis=0), NN)
 
     def fine_b(g, carry):
         s = scale_v[g]
@@ -253,7 +262,7 @@
     def convert(c, carry):
         for k in range(2):
             at = pl.multiple_of((2 * c + k) * cdev, cdev)
-            cb_v[k, c] = coarse_v[:, pl.ds(at, cdev)].astype(BF)
+            cb_v[k, c] = coarse_v[:, pl.ds(at, cdev)].astype(BF).T
         return carry
 
     lax.fori_loop(0, nch, convert, 0, unroll=2)
@@ -293,8 +302,8 @@
 
     def mid_product(mwin, g, before):
         v3 = jnp.concatenate([mwin[before + k] for k in range(3)], axis=1)
-        t3 = jnp.concatenate([mid_v[g, k] for k in range(3)], axis=1)
-        return dot(v3, t3, NT)
+        t3 = jnp.concatenate([mid_v[g, k] for k in range(3)], axis=0)
+        return dot(v3, t3, NN)
 
     mb = [None] * (nm + 2)
 
@@ -349,8 +358,8 @@
     def coarse_half(k, acc):
         def chunk(c, acc):
             v = jnp.concatenate([ag[k, 4 * c + i] for i in range(4)], axis=1)
-            t = jnp.concatenate([cb_v[k, 4 * c + i] for i in range(4)], axis=1)
-            return acc + dot(v, t, NT)
+            t = jnp.concatenate([cb_v[k, 4 * c + i] for i in range(4)], axis=0)
+            return acc + dot(v, t, NN)
 
         return lax.fori_loop(0, nch // 4, chunk, acc, unroll=nch // 4)
 

time: 62.1 us -> 58.9 us (0.948)
  Pallas kernels: 60.6 us -> 57.3 us
    pallas_call x1, Pallas kernels: 58.8 us -> 55.5 us  [on_device(): pl.pallas_call(functools.partial(kernel, ny, nz, nx), out_shape=(jax.Shap...]
where the time goes in v5:
time: 58.9 us; the launch traced here: 58 us
  Pallas kernels  57.3 us (97%)
  between operations  0.64 us (1%)
    pallas_call x1, Pallas kernels, on_device(): pl.pallas_call(functools.partial(kernel, ny, nz, nx), out_shape=(jax.Shap...  55.5 us
    pallas_call x1, Pallas kernels, on_device(): pl.pallas_call(place, out_shape=(jax.ShapeDtypeStruct((cols, n), F32), ja...  1.79 us

profile of v5, /device:TPU:1, one launch (start us, length us, event | category | flops | bytes accessed | tf_op | source)
XLA Modules:
  0.0 58.0 jit_solution(7643563270362599147)
XLA Ops:
  0.6 55.5 %vcycle.1 = (f32[16,8192]{1,0:T(8,128)}, f32[16,64]{1,0:T(8,128)}) custom-call(f32[16,8192]{1,0:T(8,128)} %bitcast.7, bf16[16,8192]{1,0:T(8,128)(2,1)} %bitcast.8, bf16[64,4,128,128]{3,2,1,0:T(8,128)(2,1)} %tiles_hbm.1, s32[4,64]{1,0:T(4,128)} %bitcast.11, bf16[8,3,128,128]{3,2,1,0:T(8,128)(2,1)} %mid_hbm.1, s32[64,128]{1,0:T(8,128)} %bitcast.9, ...), custom_call_target="tpu_custom_call" | custom-call | tf_op jit(solution)/shard_map/vcycle/pallas_call | solution.py:521
  56.2 1.8 %place.1 = (f32[16,8192]{1,0:T(8,128)}, f32[16,64]{1,0:T(8,128)}) custom-call(f32[16,8192]{1,0:T(8,128)} %get-tuple-element.6.a_ref, f32[16,64]{1,0:T(8,128)} %get-tuple-element.7.b_ref), custom_call_target="tpu_custom_call" | custom-call | tf_op jit(solution)/shard_map/place/pallas_call | solution.py:538

commit v6 on v5

--- a/solution.py
+++ b/solution.py
@@ -213,7 +213,6 @@
     for copy, when in edges:
         send(copy, when)
 
-    own_in.wait()
     low_iota = lax.broadcasted_iota(jnp.int32, (L, L), 0)
     fine_base = r * (nm * L)
 
@@ -224,8 +223,6 @@
         low = jnp.bitwise_and(owner_row(g), L - 1)
         oht[:, lanes(g)] = jnp.where(low_iota == low, 1.0, 0.0).astype(BF)
         return carry
-
-    lax.fori_loop(0, nb, hot, 0, unroll=4)
 
     off_in.wait()
 
@@ -253,9 +250,10 @@
         win2[nb + g] = v.astype(BF)
         return carry
 
-    for q in range(QUARTERS):
-        lax.fori_loop(q * step, (q + 1) * step, fine_b, 0, unroll=step)
-        halo_start(win2, 1, q * step, step)
+    ends = (0, step // 2, 3 * step // 2, 5 * step // 2, 7 * step // 2, nb)
+    for lo, hi in zip(ends, ends[1:]):
+        lax.fori_loop(lo, hi, fine_b, 0, unroll=hi - lo)
+        halo_start(win2, 1, lo, hi - lo)
 
     coarse_in.wait()
 
@@ -266,6 +264,8 @@
         return carry
 
     lax.fori_loop(0, nch, convert, 0, unroll=2)
+    own_in.wait()
+    lax.fori_loop(0, nb, hot, 0, unroll=4)
     halo_wait(win2, 1)
 
     def residual(g, carry):

time: 58.9 us -> 59.1 us (level)
  no operation moved by 1% of the time
where the time goes in v6:
time: 59.1 us; the launch traced here: 57.9 us
  Pallas kernels  57.3 us (97%)
  between operations  0.64 us (1%)
    pallas_call x1, Pallas kernels, on_device(): pl.pallas_call(functools.partial(kernel, ny, nz, nx), out_shape=(jax.Shap...  55.5 us
    pallas_call x1, Pallas kernels, on_device(): pl.pallas_call(place, out_shape=(jax.ShapeDtypeStruct((cols, n), F32), ja...  1.79 us

profile of v6, /device:TPU:1, one launch (start us, length us, event | category | flops | bytes accessed | tf_op | source)
XLA Modules:
  0.0 57.9 jit_solution(8712541984063092930)
XLA Ops:
  0.6 55.5 %vcycle.1 = (f32[16,8192]{1,0:T(8,128)}, f32[16,64]{1,0:T(8,128)}) custom-call(f32[16,8192]{1,0:T(8,128)} %bitcast.7, bf16[16,8192]{1,0:T(8,128)(2,1)} %bitcast.8, bf16[64,4,128,128]{3,2,1,0:T(8,128)(2,1)} %tiles_hbm.1, s32[4,64]{1,0:T(4,128)} %bitcast.11, bf16[8,3,128,128]{3,2,1,0:T(8,128)(2,1)} %mid_hbm.1, s32[64,128]{1,0:T(8,128)} %bitcast.9, ...), custom_call_target="tpu_custom_call" | custom-call | tf_op jit(solution)/shard_map/vcycle/pallas_call | solution.py:521
  56.1 1.8 %place.1 = (f32[16,8192]{1,0:T(8,128)}, f32[16,64]{1,0:T(8,128)}) custom-call(f32[16,8192]{1,0:T(8,128)} %get-tuple-element.6.a_ref, f32[16,64]{1,0:T(8,128)} %get-tuple-element.7.b_ref), custom_call_target="tpu_custom_call" | custom-call | tf_op jit(solution)/shard_map/place/pallas_call | solution.py:538
